TPU v7x, 512 devices: a whole 4x4x16 slice. The times are simulated.
512 devices in a mesh: ctx: 64 (over z, y), grp: 8 (over x, core).
Axes of the slice: x: 4, y: 4, z: 16, core: 2. Of those that a mesh axis runs over, the one named last changes fastest.
Arguments:
- query_in: bfloat16 [8192, 8192], P('ctx', 'grp'), may hold values from -6 to 6
- key_in: bfloat16 [8192, 8192], P('ctx', 'grp'), may hold values from -6 to 6
- value_in: bfloat16 [8192, 8192], P('ctx', 'grp'), may hold values from -6 to 6
- short_taps: float32 [3, 3, 8192], P(None, None, 'grp'), may hold values from -3 to 3
- decay_rate: float32 [16, 8192], P(None, 'grp'), may hold values from 0 to 1, as said below
- residues: float32 [16, 8192], P(None, 'grp'), may hold values from -2.5 to 2.5
- doc_lengths: int32 [32], replicated, may hold values from 1 to 2048, 8192 in all
- residual: bfloat16 [8192, 8192], P('ctx', 'grp'), may hold values from -6 to 6
- norm_gain: float32 [8192], P('grp'), may hold values from 0.5 to 1.5
Outputs:
- hidden_out: bfloat16 [8192, 8192], P('ctx', 'grp')
- normed: bfloat16 [8192, 8192], P('ctx', 'grp')
Inputs may be any that keep to these rules, and one draw needn't show every extreme that they name: `doc_lengths`: the lengths are positive, sum to 8192, and the largest is exactly 2048. `decay_rate`: positive decay rates.
All inputs are finite; a program needn't handle non-finite values.
Results may differ from a plain program's by a relative error of at most 0.0045.
Values may be sent and summed in bfloat16 or wider, within the bound.
A program may use at most 128 MiB of HBM per device.

v0:
```python
import math

import jax
import jax.numpy as jnp
from jax import lax
from jax.sharding import PartitionSpec as P

D = 8192


highest = lax.Precision.HIGHEST


def from_behind(shard, axis, by):
    count = lax.axis_size(axis)
    pairs = [(i, i + by) for i in range(count) if 0 <= i + by < count]
    return lax.ppermute(shard, axis, pairs)


def combine_maps(earlier, later):
    return (earlier[0] * later[0], later[0] * earlier[1] + later[1])


def doc_starts(doc_lengths, positions):
    starts = jnp.cumsum(doc_lengths) - doc_lengths
    return jnp.max(jnp.where(starts[None, :] <= positions[:, None], starts[None, :], 0), axis=1)


def shift_mats(row_start, positions, tok_rows):
    row_ids = jnp.arange(tok_rows, dtype=jnp.int32)
    rim_ids = jnp.arange(2, dtype=jnp.int32)
    keep_one = (row_start < positions)[:, None]
    keep_two = (row_start <= positions - 2)[:, None]
    lag_one = ((row_ids[None, :] == row_ids[:, None] - 1) & keep_one).astype(jnp.bfloat16)
    lag_two = ((row_ids[None, :] == row_ids[:, None] - 2) & keep_two).astype(jnp.bfloat16)
    rim_one = ((rim_ids[None, :] == 1) & (row_ids[:, None] == 0) & keep_one).astype(jnp.bfloat16)
    rim_two = ((rim_ids[None, :] == row_ids[:, None]) & keep_two).astype(jnp.bfloat16)
    unit = (row_ids[:, None] == row_ids[None, :]).astype(jnp.bfloat16)
    return (unit, lag_one, lag_two, rim_one, rim_two)


def rows_conv(signal, rim, taps, mats):
    unit, lag_one, lag_two, rim_one, rim_two = mats
    first = jnp.dot(lag_one, signal, preferred_element_type=jnp.float32) + jnp.dot(
        rim_one, rim, preferred_element_type=jnp.float32
    )
    second = jnp.dot(lag_two, signal, preferred_element_type=jnp.float32) + jnp.dot(
        rim_two, rim, preferred_element_type=jnp.float32
    )
    return (
        taps[0][None, :] * signal.astype(jnp.float32)
        + taps[1][None, :] * first
        + taps[2][None, :] * second
    )


def cols_conv(signal, rim, taps, mats):
    unit, lag_one, lag_two, rim_one, rim_two = mats
    own = jnp.einsum("sc,ts->ct", signal, unit, preferred_element_type=jnp.float32)
    first = jnp.einsum(
        "sc,ts->ct", signal, lag_one, preferred_element_type=jnp.float32
    ) + jnp.einsum("rc,tr->ct", rim, rim_one, preferred_element_type=jnp.float32)
    second = jnp.einsum(
        "sc,ts->ct", signal, lag_two, preferred_element_type=jnp.float32
    ) + jnp.einsum("rc,tr->ct", rim, rim_two, preferred_element_type=jnp.float32)
    return taps[0][:, None] * own + taps[1][:, None] * first + taps[2][:, None] * second


def channel_conv(gate_vals, row_start, row_pos, rate, weight):
    span_rows = 128
    channels, length = gate_vals.shape
    block_count = length // span_rows
    lag_ids = jnp.arange(span_rows, dtype=jnp.float32)
    decay_table = jnp.exp(-lag_ids[None, None, :] * rate[:, :, None])
    step_table = jnp.exp(-(lag_ids[None, None, :] + 1.0) * rate[:, :, None]) * weight[:, :, None]
    lag_grid = jnp.maximum(lag_ids[:, None] - lag_ids[None, :], 0.0)
    lower = (lag_ids[:, None] >= lag_ids[None, :]).astype(jnp.float32)
    toeplitz = jnp.zeros((channels, span_rows, span_rows), jnp.float32)
    for mode in range(rate.shape[1]):
        toeplitz = toeplitz + weight[:, mode, None, None] * jnp.exp(
            -rate[:, mode, None, None] * lag_grid[None]
        )
    toeplitz = toeplitz * lower[None]
    blocked = gate_vals.reshape(channels, block_count, span_rows)
    start_blk = row_start.reshape(block_count, span_rows)
    pos_blk = row_pos.reshape(block_count, span_rows)
    inside = (start_blk < pos_blk[:, :1]).astype(jnp.float32)
    group_size = math.gcd(block_count, 8)
    group_count = block_count // group_size

    def intra_group(index):
        gate_grp = lax.dynamic_slice_in_dim(blocked, index * group_size, group_size, 1)
        start_grp = lax.dynamic_slice_in_dim(start_blk, index * group_size, group_size, 0)
        pos_grp = lax.dynamic_slice_in_dim(pos_blk, index * group_size, group_size, 0)
        same_doc = (pos_grp[:, None, :] >= start_grp[:, :, None]).astype(jnp.float32)
        return jnp.sum(toeplitz[:, None] * same_doc[None] * gate_grp[:, :, None, :], axis=3)

    intra = lax.map(intra_group, jnp.arange(group_count, dtype=jnp.int32))
    intra = intra.transpose(1, 0, 2, 3).reshape(channels, block_count, span_rows)
    end_mask = (pos_blk >= start_blk[:, span_rows - 1 :]).astype(jnp.float32)
    block_ends = jnp.einsum(
        "cnj,cbj->cnb", decay_table[:, :, ::-1], blocked * end_mask[None], precision=highest
    )
    carried = jnp.exp(-float(span_rows) * rate)[:, :, None] * inside[None, None, :, span_rows - 1]
    prefix_maps = lax.associative_scan(combine_maps, (carried, block_ends), axis=2)
    entering = jnp.concatenate(
        [jnp.zeros((channels, rate.shape[1], 1), jnp.float32), prefix_maps[1][:, :, :-1]], axis=2
    )
    from_state = jnp.einsum("cni,cnb->cbi", step_table, entering, precision=highest)
    result = intra + from_state * inside[None]
    return result.reshape(channels, length)


def shards(
    query_in, key_in, value_in, short_taps, decay_rate, residues, doc_lengths, residual, norm_gain
):
    tok_rows = query_in.shape[0]
    ctx_index = lax.axis_index("ctx")
    tails = jnp.stack([query_in[tok_rows - 2 :], key_in[tok_rows - 2 :], value_in[tok_rows - 2 :]])
    rim_rows = from_behind(tails, "ctx", 1)
    positions = ctx_index * tok_rows + jnp.arange(tok_rows, dtype=jnp.int32)
    row_start = doc_starts(doc_lengths, positions)
    mats = shift_mats(row_start, positions, tok_rows)
    q_short = rows_conv(query_in, rim_rows[0], short_taps[0], mats)
    weight = residues * jnp.sqrt(-jnp.expm1(-2.0 * decay_rate))
    k_cols = cols_conv(key_in, rim_rows[1], short_taps[1], mats)
    v_cols = cols_conv(value_in, rim_rows[2], short_taps[2], mats)
    gate_cols = (k_cols * v_cols).astype(jnp.bfloat16)
    moved = lax.all_to_all(gate_cols, "ctx", split_axis=0, concat_axis=1, tiled=True)
    few_chans = moved.shape[0]
    all_rows = moved.shape[1]
    all_pos = jnp.arange(all_rows, dtype=jnp.int32)
    all_start = doc_starts(doc_lengths, all_pos)
    rate_few = lax.dynamic_slice_in_dim(decay_rate, ctx_index * few_chans, few_chans, 1).T
    weight_few = lax.dynamic_slice_in_dim(weight, ctx_index * few_chans, few_chans, 1).T
    conv_few = channel_conv(moved.astype(jnp.float32), all_start, all_pos, rate_few, weight_few)
    returned = lax.all_to_all(
        conv_few.astype(jnp.bfloat16), "ctx", split_axis=1, concat_axis=0, tiled=True
    )
    conv_out = returned.T
    hidden = residual.astype(jnp.float32) + q_short * conv_out.astype(jnp.float32)
    square_sum = lax.psum(jnp.sum(hidden * hidden, axis=1), "grp")
    inverse_rms = lax.rsqrt(square_sum / D + 1e-06)
    normed = (hidden * inverse_rms[:, None] * norm_gain[None, :]).astype(jnp.bfloat16)
    return (hidden.astype(jnp.bfloat16), normed)


def solution(mesh):
    return jax.shard_map(
        shards,
        mesh=mesh,
        in_specs=(
            P("ctx", "grp"),
            P("ctx", "grp"),
            P("ctx", "grp"),
            P(None, None, "grp"),
            P(None, "grp"),
            P(None, "grp"),
            P(),
            P("ctx", "grp"),
            P("grp"),
        ),
        out_specs=(P("ctx", "grp"), P("ctx", "grp")),
        check_vma=False,
    )
```

profile of v0, /device:TPU:1, one launch (start us, length us, event | category | flops | bytes accessed | tf_op | source)
XLA Modules:
  0.0 186.8 jit_solution(8396714889131522424)
XLA Ops:
  2.2 4.0 %collective-permute-start = (bf16[3,2,1024]{2,1,0:T(2,128)(2,1)S(1)}, bf16[3,2,1024]{2,1,0:T(2,128)(2,1)S(1)}, u32[]{:S(2)}, u32[]{:S(2)}) collective-permute-start(bf16[3,2,1024]{2,1,0:T(2,128)(2,1)S(1)} %pad_maximum_fusion.5), channel_id=1, source_target_pairs={{0,8},{8,16},{16,24},{24,32},{32,40},{40,48},{48,56},{56,64},{64,7... | collective-permute-start | bytes 36872 | tf_op jit(solution)/shard_map/ppermute | solution.py:17
  16.5 18.3 %all-to-all-start = ((bf16[64,16,128]{2,1,0:T(8,128)(2,1)}), bf16[64,16,128]{2,1,0:T(8,128)(2,1)S(1)}, u32[]{:S(2)}, u32[]{:S(2)}) async-start(bf16[64,16,128]{2,1,0:T(8,128)(2,1)} %bitcast.23), calls=%async_computation | async-start | bytes 524288 | tf_op jit(solution)/shard_map/all_to_all | solution.py:129
  34.9 1.3 slice.361
  36.2 1.2 slice.365
  39.2 14.8 %all-to-all-done = bf16[64,16,128]{2,1,0:T(8,128)(2,1)S(1)} async-done(((bf16[64,16,128]{2,1,0:T(8,128)(2,1)}), bf16[64,16,128]{2,1,0:T(8,128)(2,1)S(1)}, u32[]{:S(2)}, u32[]{:S(2)}) %all-to-all-start) | async-done | bytes 262176 | tf_op jit(solution)/shard_map/all_to_all | solution.py:129
  56.4 1.3 slice.363
  74.7 1.4 pad.45
  76.2 1.3 pad.44
  77.7 1.6 pad.46
  79.3 1.6 pad.47
  81.0 2.2 %pad.83 = f32[16,16,64]{2,1,0:T(8,128)S(1)} pad(f32[16,16,32]{2,1,0:T(8,128)S(1)} %add.277, f32[]{:T(128)} %constant.25.clone.1), padding=0_0_0x0_0_0x1_0_1 | pad | bytes 98308
  83.3 2.1 %pad.64 = f32[16,16,63]{2,1,0:T(8,128)S(1)} pad(f32[16,16,32]{2,1,0:T(8,128)S(1)} %pad_maximum_fusion.4, f32[]{:T(128)} %constant.25.clone.1), padding=0_0_0x0_0_0x0_0_1 | pad | bytes 97284 | tf_op jit(solution)/shard_map/slice | solution.py:107
  85.5 54.9 %while.11 = (s32[]{:T(128)}, f32[8,16,8,128]{3,2,1,0:T(8,128)S(1)}, s32[8]{0:T(128)S(1)}, s32[64,128]{1,0:T(8,128)S(1)}, s32[64,128]{1,0:T(8,128)S(1)}, /*index=...) while((s32[]{:T(128)}, f32[8,16,8,128]{3,2,1,0:T(8,128)S(1)}, ...), condition=%wide.region_5.6_spmd.clone, body=%wide.region_3.5_spmd.clone.sunk | while | flops 19120132 | bytes 3828155 | solution.py:98
  87.2 3.0 %add_multiply_fusion.7 = f32[16,128,128]{2,1,0:T(8,128)S(1)} fusion(f32[128,128]{1,0:T(8,128)S(1)} %get-tuple-element.794, f32[16]{0:T(128)S(1)} %get-tuple-element.792, f32[16]{0:T(128)S(1)} %get-tuple-element.793, f32[16]{0:T(128)S(1)} %get-tuple-element.789, f32[16]{0:T(128)S(1)} %get-tuple-element.790, f32[16]{0:T(128)S(1)} %get-tuple-element.787, ...), kind=kLoop, calls=%fused_computation.2.clone.1 | loop fusion | flops 12582912 | bytes 1181696 | tf_op jit(solution)/shard_map/mul | solution.py:83
  90.3 2.2 %multiply_reduce_fusion.3 = f32[16,8,128]{2,1,0:T(8,128)S(1)} fusion(f32[16,8,128]{2,1,0:T(8,128)S(1)} %copy.80, f32[8,128,128]{2,1,0:T(8,128)S(1)} %compare_convert_fusion.4, f32[16,128,128]{2,1,0:T(8,128)S(1)} %add_multiply_fusion.7), kind=kLoop, calls=%fused_computation.1.clone.1 | loop fusion | flops 6275072 | bytes 1703936 | tf_op jit(solution)/shard_map/while/body/eval_jaxpr/reduce_sum | solution.py:96
  94.0 3.0 %add_multiply_fusion.7 = f32[16,128,128]{2,1,0:T(8,128)S(1)} fusion(f32[128,128]{1,0:T(8,128)S(1)} %get-tuple-element.794, f32[16]{0:T(128)S(1)} %get-tuple-element.792, f32[16]{0:T(128)S(1)} %get-tuple-element.793, f32[16]{0:T(128)S(1)} %get-tuple-element.789, f32[16]{0:T(128)S(1)} %get-tuple-element.790, f32[16]{0:T(128)S(1)} %get-tuple-element.787, ...), kind=kLoop, calls=%fused_computation.2.clone.1 | loop fusion | flops 12582912 | bytes 1181696 | tf_op jit(solution)/shard_map/mul | solution.py:83
  97.1 2.2 %multiply_reduce_fusion.3 = f32[16,8,128]{2,1,0:T(8,128)S(1)} fusion(f32[16,8,128]{2,1,0:T(8,128)S(1)} %copy.80, f32[8,128,128]{2,1,0:T(8,128)S(1)} %compare_convert_fusion.4, f32[16,128,128]{2,1,0:T(8,128)S(1)} %add_multiply_fusion.7), kind=kLoop, calls=%fused_computation.1.clone.1 | loop fusion | flops 6275072 | bytes 1703936 | tf_op jit(solution)/shard_map/while/body/eval_jaxpr/reduce_sum | solution.py:96
  100.9 3.0 %add_multiply_fusion.7 = f32[16,128,128]{2,1,0:T(8,128)S(1)} fusion(f32[128,128]{1,0:T(8,128)S(1)} %get-tuple-element.794, f32[16]{0:T(128)S(1)} %get-tuple-element.792, f32[16]{0:T(128)S(1)} %get-tuple-element.793, f32[16]{0:T(128)S(1)} %get-tuple-element.789, f32[16]{0:T(128)S(1)} %get-tuple-element.790, f32[16]{0:T(128)S(1)} %get-tuple-element.787, ...), kind=kLoop, calls=%fused_computation.2.clone.1 | loop fusion | flops 12582912 | bytes 1181696 | tf_op jit(solution)/shard_map/mul | solution.py:83
  104.0 2.2 %multiply_reduce_fusion.3 = f32[16,8,128]{2,1,0:T(8,128)S(1)} fusion(f32[16,8,128]{2,1,0:T(8,128)S(1)} %copy.80, f32[8,128,128]{2,1,0:T(8,128)S(1)} %compare_convert_fusion.4, f32[16,128,128]{2,1,0:T(8,128)S(1)} %add_multiply_fusion.7), kind=kLoop, calls=%fused_computation.1.clone.1 | loop fusion | flops 6275072 | bytes 1703936 | tf_op jit(solution)/shard_map/while/body/eval_jaxpr/reduce_sum | solution.py:96
  107.7 3.0 %add_multiply_fusion.7 = f32[16,128,128]{2,1,0:T(8,128)S(1)} fusion(f32[128,128]{1,0:T(8,128)S(1)} %get-tuple-element.794, f32[16]{0:T(128)S(1)} %get-tuple-element.792, f32[16]{0:T(128)S(1)} %get-tuple-element.793, f32[16]{0:T(128)S(1)} %get-tuple-element.789, f32[16]{0:T(128)S(1)} %get-tuple-element.790, f32[16]{0:T(128)S(1)} %get-tuple-element.787, ...), kind=kLoop, calls=%fused_computation.2.clone.1 | loop fusion | flops 12582912 | bytes 1181696 | tf_op jit(solution)/shard_map/mul | solution.py:83
  110.8 2.2 %multiply_reduce_fusion.3 = f32[16,8,128]{2,1,0:T(8,128)S(1)} fusion(f32[16,8,128]{2,1,0:T(8,128)S(1)} %copy.80, f32[8,128,128]{2,1,0:T(8,128)S(1)} %compare_convert_fusion.4, f32[16,128,128]{2,1,0:T(8,128)S(1)} %add_multiply_fusion.7), kind=kLoop, calls=%fused_computation.1.clone.1 | loop fusion | flops 6275072 | bytes 1703936 | tf_op jit(solution)/shard_map/while/body/eval_jaxpr/reduce_sum | solution.py:96
  114.5 3.0 %add_multiply_fusion.7 = f32[16,128,128]{2,1,0:T(8,128)S(1)} fusion(f32[128,128]{1,0:T(8,128)S(1)} %get-tuple-element.794, f32[16]{0:T(128)S(1)} %get-tuple-element.792, f32[16]{0:T(128)S(1)} %get-tuple-element.793, f32[16]{0:T(128)S(1)} %get-tuple-element.789, f32[16]{0:T(128)S(1)} %get-tuple-element.790, f32[16]{0:T(128)S(1)} %get-tuple-element.787, ...), kind=kLoop, calls=%fused_computation.2.clone.1 | loop fusion | flops 12582912 | bytes 1181696 | tf_op jit(solution)/shard_map/mul | solution.py:83
  117.6 2.2 %multiply_reduce_fusion.3 = f32[16,8,128]{2,1,0:T(8,128)S(1)} fusion(f32[16,8,128]{2,1,0:T(8,128)S(1)} %copy.80, f32[8,128,128]{2,1,0:T(8,128)S(1)} %compare_convert_fusion.4, f32[16,128,128]{2,1,0:T(8,128)S(1)} %add_multiply_fusion.7), kind=kLoop, calls=%fused_computation.1.clone.1 | loop fusion | flops 6275072 | bytes 1703936 | tf_op jit(solution)/shard_map/while/body/eval_jaxpr/reduce_sum | solution.py:96
  121.4 3.0 %add_multiply_fusion.7 = f32[16,128,128]{2,1,0:T(8,128)S(1)} fusion(f32[128,128]{1,0:T(8,128)S(1)} %get-tuple-element.794, f32[16]{0:T(128)S(1)} %get-tuple-element.792, f32[16]{0:T(128)S(1)} %get-tuple-element.793, f32[16]{0:T(128)S(1)} %get-tuple-element.789, f32[16]{0:T(128)S(1)} %get-tuple-element.790, f32[16]{0:T(128)S(1)} %get-tuple-element.787, ...), kind=kLoop, calls=%fused_computation.2.clone.1 | loop fusion | flops 12582912 | bytes 1181696 | tf_op jit(solution)/shard_map/mul | solution.py:83
  124.5 2.2 %multiply_reduce_fusion.3 = f32[16,8,128]{2,1,0:T(8,128)S(1)} fusion(f32[16,8,128]{2,1,0:T(8,128)S(1)} %copy.80, f32[8,128,128]{2,1,0:T(8,128)S(1)} %compare_convert_fusion.4, f32[16,128,128]{2,1,0:T(8,128)S(1)} %add_multiply_fusion.7), kind=kLoop, calls=%fused_computation.1.clone.1 | loop fusion | flops 6275072 | bytes 1703936 | tf_op jit(solution)/shard_map/while/body/eval_jaxpr/reduce_sum | solution.py:96
  128.2 3.0 %add_multiply_fusion.7 = f32[16,128,128]{2,1,0:T(8,128)S(1)} fusion(f32[128,128]{1,0:T(8,128)S(1)} %get-tuple-element.794, f32[16]{0:T(128)S(1)} %get-tuple-element.792, f32[16]{0:T(128)S(1)} %get-tuple-element.793, f32[16]{0:T(128)S(1)} %get-tuple-element.789, f32[16]{0:T(128)S(1)} %get-tuple-element.790, f32[16]{0:T(128)S(1)} %get-tuple-element.787, ...), kind=kLoop, calls=%fused_computation.2.clone.1 | loop fusion | flops 12582912 | bytes 1181696 | tf_op jit(solution)/shard_map/mul | solution.py:83
  131.3 2.2 %multiply_reduce_fusion.3 = f32[16,8,128]{2,1,0:T(8,128)S(1)} fusion(f32[16,8,128]{2,1,0:T(8,128)S(1)} %copy.80, f32[8,128,128]{2,1,0:T(8,128)S(1)} %compare_convert_fusion.4, f32[16,128,128]{2,1,0:T(8,128)S(1)} %add_multiply_fusion.7), kind=kLoop, calls=%fused_computation.1.clone.1 | loop fusion | flops 6275072 | bytes 1703936 | tf_op jit(solution)/shard_map/while/body/eval_jaxpr/reduce_sum | solution.py:96
  135.1 3.0 %add_multiply_fusion.7 = f32[16,128,128]{2,1,0:T(8,128)S(1)} fusion(f32[128,128]{1,0:T(8,128)S(1)} %get-tuple-element.794, f32[16]{0:T(128)S(1)} %get-tuple-element.792, f32[16]{0:T(128)S(1)} %get-tuple-element.793, f32[16]{0:T(128)S(1)} %get-tuple-element.789, f32[16]{0:T(128)S(1)} %get-tuple-element.790, f32[16]{0:T(128)S(1)} %get-tuple-element.787, ...), kind=kLoop, calls=%fused_computation.2.clone.1 | loop fusion | flops 12582912 | bytes 1181696 | tf_op jit(solution)/shard_map/mul | solution.py:83
  138.2 2.2 %multiply_reduce_fusion.3 = f32[16,8,128]{2,1,0:T(8,128)S(1)} fusion(f32[16,8,128]{2,1,0:T(8,128)S(1)} %copy.80, f32[8,128,128]{2,1,0:T(8,128)S(1)} %compare_convert_fusion.4, f32[16,128,128]{2,1,0:T(8,128)S(1)} %add_multiply_fusion.7), kind=kLoop, calls=%fused_computation.1.clone.1 | loop fusion | flops 6275072 | bytes 1703936 | tf_op jit(solution)/shard_map/while/body/eval_jaxpr/reduce_sum | solution.py:96
  142.5 7.2 %all-to-all-start.1 = ((bf16[16,64,128]{2,0,1:T(8,128)(2,1)}), bf16[16,64,128]{2,0,1:T(8,128)(2,1)S(1)}, u32[]{:S(2)}, u32[]{:S(2)}) async-start(bf16[16,64,128]{2,0,1:T(8,128)(2,1)} %copy.69), calls=%async_computation.1 | async-start | bytes 524288 | tf_op jit(solution)/shard_map/all_to_all | solution.py:137
  150.6 17.8 %all-to-all-done.1 = bf16[16,64,128]{2,0,1:T(8,128)(2,1)S(1)} async-done(((bf16[16,64,128]{2,0,1:T(8,128)(2,1)}), bf16[16,64,128]{2,0,1:T(8,128)(2,1)S(1)}, u32[]{:S(2)}, u32[]{:S(2)}) %all-to-all-start.1) | async-done | bytes 262176 | tf_op jit(solution)/shard_map/all_to_all | solution.py:137
  169.1 16.8 %psum.7 = f32[128]{0:T(128)S(1)} all-reduce(f32[128]{0:T(128)S(1)} %get-tuple-element.417), channel_id=1, replica_groups=mesh['ctx'=64,'grp'=8] {'grp'}, use_global_device_ids=true, to_apply=%region_7.8 | all-reduce | flops 128 | bytes 1024 | tf_op jit(solution)/shard_map/psum | solution.py:142
  (175 shorter events, 44.1 us)
Async XLA Ops:
  0.6 8.9 %copy-start = (bf16[128,1024]{1,0:T(8,128)(2,1)S(1)}, bf16[128,1024]{1,0:T(8,128)(2,1)}, u32[]{:S(2)}) copy-start(bf16[128,1024]{1,0:T(8,128)(2,1)} %param.13) | copy-start | bytes 786436
  0.6 8.5 %copy-start.1 = (bf16[128,1024]{1,0:T(8,128)(2,1)S(1)}, bf16[128,1024]{1,0:T(8,128)(2,1)}, u32[]{:S(2)}) copy-start(bf16[128,1024]{1,0:T(8,128)(2,1)} %param.12) | copy-start | bytes 786436
  2.2 11.8 %collective-permute-start = (bf16[3,2,1024]{2,1,0:T(2,128)(2,1)S(1)}, bf16[3,2,1024]{2,1,0:T(2,128)(2,1)S(1)}, u32[]{:S(2)}, u32[]{:S(2)}) collective-permute-start(bf16[3,2,1024]{2,1,0:T(2,128)(2,1)S(1)} %pad_maximum_fusion.5), channel_id=1, source_target_pairs={{0,8},{8,16},{16,24},{24,32},{32,40},{40,48},{48,56},{56,64},{64,7... | collective-permute-start | bytes 36872 | tf_op jit(solution)/shard_map/ppermute | solution.py:17
  9.2 1.2 copy-start.5
  14.0 1.0 copy-start.3
  16.5 37.5 %all-to-all-start = ((bf16[64,16,128]{2,1,0:T(8,128)(2,1)}), bf16[64,16,128]{2,1,0:T(8,128)(2,1)S(1)}, u32[]{:S(2)}, u32[]{:S(2)}) async-start(bf16[64,16,128]{2,1,0:T(8,128)(2,1)} %bitcast.23), calls=%async_computation | async-start | bytes 524288 | tf_op jit(solution)/shard_map/all_to_all | solution.py:129
  140.5 9.3 %copy-start.2 = (bf16[128,1024]{1,0:T(8,128)(2,1)S(1)}, bf16[128,1024]{1,0:T(8,128)(2,1)}, u32[]{:S(2)}) copy-start(bf16[128,1024]{1,0:T(8,128)(2,1)} %param.11) | copy-start | bytes 786436
  142.5 25.9 %all-to-all-start.1 = ((bf16[16,64,128]{2,0,1:T(8,128)(2,1)}), bf16[16,64,128]{2,0,1:T(8,128)(2,1)S(1)}, u32[]{:S(2)}, u32[]{:S(2)}) async-start(bf16[16,64,128]{2,0,1:T(8,128)(2,1)} %copy.69), calls=%async_computation.1 | async-start | bytes 524288 | tf_op jit(solution)/shard_map/all_to_all | solution.py:137
  150.6 18.1 %copy-start.4 = (bf16[128,1024]{1,0:T(8,128)(2,1)S(1)}, bf16[128,1024]{1,0:T(8,128)(2,1)}, u32[]{:S(2)}) copy-start(bf16[128,1024]{1,0:T(8,128)(2,1)} %param.18) | copy-start | bytes 786436
  168.7 17.2 %copy-start.6 = (f32[1024]{0:T(1024)S(1)}, f32[1024]{0:T(1024)}, u32[]{:S(2)}) copy-start(f32[1024]{0:T(1024)} %param.19) | copy-start | bytes 12292
where the time goes:
time: 187 us
  other arithmetic  49.4 us (26%)
  local copies, waits for them, and re-layouts  43 us (23%)
  waiting for transfers between devices  32.7 us (17%)
  starting transfers between devices  29.6 us (16%)
  blocking collectives  16.8 us (9%)
  matrix products  7.82 us (4%)
  loops' own time  6 us (3%)
    mul x8, other arithmetic, channel_conv(): toeplitz = toeplitz * lower[None]  24.3 us
    all_to_all x1, starting transfers between devices, shards(): lax.all_to_all(gate_cols, 'ctx', split_axis=0, concat_axis=1, tiled=True)  18.3 us
    reduce_sum x8, other arithmetic, intra_group(): jnp.sum(toeplitz[:, None] * same_doc[None] * gate_grp[:, :, None, :], axi...  17.9 us
    all_to_all x1, waiting for transfers between devices, shards(): lax.all_to_all(conv_few.astype(jnp.bfloat16), 'ctx', split_axis=1, concat...  17.8 us
    slice x28, local copies, waits for them, and re-layouts, channel_conv(): lax.associative_scan(combine_maps, (carried, block_ends), axis=2)  17.5 us
    psum x1, blocking collectives, shards(): square_sum = lax.psum(jnp.sum(hidden * hidden, axis=1), 'grp')  16.8 us
    all_to_all x1, waiting for transfers between devices, shards(): lax.all_to_all(gate_cols, 'ctx', split_axis=0, concat_axis=1, tiled=True)  14.8 us
    pad x8, local copies, waits for them, and re-layouts, channel_conv(): lax.associative_scan(combine_maps, (carried, block_ends), axis=2)  10.6 us
  transfers between devices with their start and end apart: 3, of which 2 were waited for; matrix products, arithmetic and copies ran while one was open for 7% of the time, Pallas kernels for 0%

commit v1 on v0

v1 whole, which is shorter than its diff:
```python
import functools

import jax
import jax.numpy as jnp
from jax import lax
from jax.experimental import pallas as pl
from jax.experimental.pallas import tpu as pltpu
from jax.sharding import PartitionSpec as P

D = 8192
MESH = pl.DeviceIdType.MESH
F32 = jnp.float32
BF16 = jnp.bfloat16
YN = 4
BACK = 4


def decay_weight(rate, residue):
    x = 2.0 * rate
    series = 1.0 - x / 8.0
    for k in (7.0, 6.0, 5.0, 4.0, 3.0, 2.0):
        series = 1.0 - (x / k) * series
    one_minus = jnp.where(x < 0.25, x * series, 1.0 - jnp.exp(-x))
    return residue * jnp.sqrt(one_minus)


def block_kernel(
    nctx,
    ngrp,
    doc_ref,
    q_ref,
    k_ref,
    v_ref,
    taps_ref,
    rate_ref,
    res_ref,
    resid_ref,
    gain_ref,
    hid_ref,
    norm_ref,
    tail_ref,
    halo_ref,
    qs_ref,
    g_ref,
    y_ref,
    keep_ref,
    pre_ref,
    carry_ref,
    nat_ref,
    a_ref,
    w_ref,
    rate3_ref,
    e_ref,
    r1_ref,
    t_ref,
    r2_ref,
    i_ref,
    r3_ref,
    ss_ref,
    rs_ref,
    halo_send,
    halo_recv,
    s1,
    v1,
    s2,
    v2,
    s3,
    v3,
    s4,
    v4,
):
    tok, chans = q_ref.shape
    lanes = 128
    tiles = chans // lanes
    modes = rate_ref.shape[0]
    ndoc = doc_ref.shape[0]
    quarter = modes // YN
    zn = nctx // YN
    me = lax.axis_index("ctx")
    gi = lax.axis_index("grp")
    z = me // YN
    yy = lax.rem(me, YN)

    def in_plane(k):
        return z * YN + lax.rem(yy + k, YN)

    def plane(k):
        return lax.rem(z + k + zn, zn) * YN + yy

    barrier = pltpu.get_barrier_semaphore()
    pl.semaphore_signal(
        barrier, inc=1, device_id={"ctx": lax.rem(me + nctx - 1, nctx)}, device_id_type=MESH
    )
    for k in range(1, YN):
        pl.semaphore_signal(
            barrier, inc=1, device_id={"ctx": in_plane(YN - k)}, device_id_type=MESH
        )
    for k in range(1, BACK + 1):
        pl.semaphore_signal(barrier, inc=1, device_id={"ctx": plane(-k)}, device_id_type=MESH)
    for k in range(1, ngrp):
        pl.semaphore_signal(
            barrier, inc=1, device_id={"grp": lax.rem(gi + ngrp - k, ngrp)}, device_id_type=MESH
        )

    for i, ref in enumerate((q_ref, k_ref, v_ref)):
        tail_ref[2 * i : 2 * i + 2, :] = ref[tok - 16 :, :].astype(F32)[14:16]
    tail_ref[6:8, :] = jnp.zeros((2, chans), F32)

    rate = rate_ref[...]
    for slot, value, dest in (
        (0, jnp.exp(-rate), a_ref),
        (1, decay_weight(rate, res_ref[...]), w_ref),
        (2, rate, rate3_ref),
    ):
        for j in range(tiles):
            nat_ref[slot, j * modes : (j + 1) * modes, :] = value[:, j * lanes : (j + 1) * lanes]
        for n in range(modes):
            dest[n] = nat_ref[slot, pl.ds(n, tiles, stride=modes), :]

    row = lax.broadcasted_iota(jnp.int32, (tok, lanes), 0)
    brow = lax.broadcasted_iota(jnp.int32, (nctx, lanes), 0)
    p0 = me * tok
    start = jnp.int32(0)
    first = jnp.int32(tok)
    before = jnp.int32(0)
    fresh = jnp.zeros((tok, lanes), F32)
    opens = jnp.zeros((nctx, lanes), F32)
    for d in range(ndoc):
        rel = start - p0
        fresh = jnp.where(row == rel, 1.0, fresh)
        opens = jnp.where(brow == start // tok, 1.0, opens)
        before = jnp.where(rel == -1, 1, before)
        first = jnp.where(rel >= 0, jnp.minimum(first, rel), first)
        start = start + doc_ref[d]
    keep_one = 1.0 - fresh
    keep_ref[...] = keep_one
    pre_ref[...] = jnp.where(row < first, 1.0, 0.0)
    carry_ref[...] = 1.0 - opens
    keep_prev = jnp.where(row == 0, (1 - before).astype(F32), pltpu.roll(keep_one, 1, 0))
    keep_two = keep_one * keep_prev

    pl.semaphore_wait(barrier, 1 + (YN - 1) + BACK + (ngrp - 1))

    halo = pltpu.make_async_remote_copy(
        src_ref=tail_ref,
        dst_ref=halo_ref,
        send_sem=halo_send,
        recv_sem=halo_recv,
        device_id={"ctx": lax.rem(me + 1, nctx)},
        device_id_type=MESH,
    )
    halo.start()
    halo.wait()

    def short(ref, i, j):
        cols = slice(j * lanes, (j + 1) * lanes)
        x = ref[:, cols].astype(F32)
        h0 = halo_ref[2 * i : 2 * i + 1, cols]
        h1 = halo_ref[2 * i + 1 : 2 * i + 2, cols]
        one = jnp.where(row == 0, h1, pltpu.roll(x, 1, 0)) * keep_one
        two = jnp.where(row == 0, h0, jnp.where(row == 1, h1, pltpu.roll(x, 2, 0))) * keep_two
        return (
            taps_ref[i, 0:1, cols] * x + taps_ref[i, 1:2, cols] * one + taps_ref[i, 2:3, cols] * two
        )

    for j in range(tiles):
        gate = short(k_ref, 1, j) * short(v_ref, 2, j)
        g_ref[j * tok : (j + 1) * tok, :] = gate.astype(BF16).astype(F32)

    def scan_step(t, states):
        g = g_ref[pl.ds(t, tiles, stride=tok), :]
        keep = keep_ref[pl.ds(t, 1), :]
        new = []
        total = None
        for n in range(modes):
            s = (a_ref[n] * keep) * states[n] + g
            term = w_ref[n] * s
            total = term if total is None else total + term
            new.append(s)
        y_ref[pl.ds(t, tiles, stride=tok), :] = total
        return tuple(new)

    zero = jnp.zeros((tiles, lanes), F32)
    states = lax.fori_loop(0, tok, scan_step, (zero,) * modes, unroll=4)
    for n in range(modes):
        e_ref[n] = states[n]

    sends = []
    for k in range(1, YN):
        to = lax.rem(yy + k, YN)
        sends.append(
            pltpu.make_async_remote_copy(
                src_ref=e_ref.at[pl.ds(to * quarter, quarter)],
                dst_ref=r1_ref.at[k],
                send_sem=s1.at[k],
                recv_sem=v1.at[k],
                device_id={"ctx": in_plane(k)},
                device_id_type=MESH,
            )
        )
    for copy in sends:
        copy.start()
    r1_ref[0] = e_ref[pl.ds(yy * quarter, quarter)]
    for j in range(tiles):
        qs_ref[j * tok : (j + 1) * tok, :] = short(q_ref, 0, j)
    rate_q = rate3_ref[pl.ds(yy * quarter, quarter)]
    decay_blk = jnp.exp(-float(tok) * rate_q)
    decay_plane = jnp.exp(-float(tok * YN) * rate_q)

    def carry_of(block):
        return carry_ref[pl.ds(block, 1), :][None]

    def plane_carry(k):
        base = lax.rem(z - k + zn, zn) * YN
        value = carry_of(base)
        for j in range(1, YN):
            value = value * carry_of(base + j)
        return value

    for copy in sends:
        copy.wait()

    ends = [r1_ref[lax.rem(yy - j + YN, YN)] for j in range(YN)]
    total = ends[0]
    for j in range(1, YN):
        total = ends[j] + decay_blk * carry_of(z * YN + j) * total
    t_ref[...] = total

    sends = []
    for k in range(1, BACK + 1):
        sends.append(
            pltpu.make_async_remote_copy(
                src_ref=t_ref,
                dst_ref=r2_ref.at[k - 1],
                send_sem=s2.at[k - 1],
                recv_sem=v2.at[k - 1],
                device_id={"ctx": plane(k)},
                device_id_type=MESH,
            )
        )
    for copy in sends:
        copy.start()
    for copy in sends:
        copy.wait()
    enter = r2_ref[BACK - 1]
    for k in range(BACK - 1, 0, -1):
        enter = r2_ref[k - 1] + decay_plane * plane_carry(k) * enter
    for j in range(YN):
        i_ref[j] = enter
        if j < YN - 1:
            enter = ends[j] + decay_blk * carry_of(z * YN + j) * enter

    sends = []
    for k in range(1, YN):
        to = lax.rem(yy + k, YN)
        sends.append(
            pltpu.make_async_remote_copy(
                src_ref=i_ref.at[to],
                dst_ref=r3_ref.at[k],
                send_sem=s3.at[k],
                recv_sem=v3.at[k],
                device_id={"ctx": in_plane(k)},
                device_id_type=MESH,
            )
        )
    for copy in sends:
        copy.start()
    r3_ref[0] = i_ref[yy]
    for copy in sends:
        copy.wait()

    entering = []
    for m in range(YN):
        part = r3_ref[lax.rem(yy - m + YN, YN)]
        for n in range(quarter):
            entering.append(w_ref[m * quarter + n] * part[n])

    def fix_step(t, states):
        new = []
        total = None
        for n in range(modes):
            s = a_ref[n] * states[n]
            total = s if total is None else total + s
            new.append(s)
        at = pl.ds(t, tiles, stride=tok)
        y_ref[at, :] = y_ref[at, :] + pre_ref[pl.ds(t, 1), :] * total
        return tuple(new)

    lax.fori_loop(0, tok, fix_step, tuple(entering), unroll=4)

    squares = jnp.zeros((tok, lanes), F32)
    for j in range(tiles):
        rows = slice(j * tok, (j + 1) * tok)
        cols = slice(j * lanes, (j + 1) * lanes)
        conv = y_ref[rows, :].astype(BF16).astype(F32)
        hidden = resid_ref[:, cols].astype(F32) + qs_ref[rows, :] * conv
        squares = squares + hidden * hidden
        qs_ref[rows, :] = hidden
        hid_ref[:, cols] = hidden.astype(BF16)
    by_token = jnp.sum(squares.T, axis=0, keepdims=True)
    ss_ref[...] = jnp.broadcast_to(by_token, (8, lanes))
    sends = []
    for k in range(1, ngrp):
        sends.append(
            pltpu.make_async_remote_copy(
                src_ref=ss_ref,
                dst_ref=rs_ref.at[k],
                send_sem=s4.at[k],
                recv_sem=v4.at[k],
                device_id={"grp": lax.rem(gi + k, ngrp)},
                device_id_type=MESH,
            )
        )
    for copy in sends:
        copy.start()
    for copy in sends:
        copy.wait()
    total = ss_ref[...]
    for k in range(1, ngrp):
        total = total + rs_ref[k]
    inverse = lax.rsqrt(total * (1.0 / D) + 1e-06)
    inverse = jnp.broadcast_to(inverse[0:1, :], (lanes, tok)).T
    for j in range(tiles):
        rows = slice(j * tok, (j + 1) * tok)
        cols = slice(j * lanes, (j + 1) * lanes)
        norm_ref[:, cols] = (qs_ref[rows, :] * inverse * gain_ref[:, cols]).astype(BF16)


def shards(
    nctx,
    ngrp,
    query_in,
    key_in,
    value_in,
    short_taps,
    decay_rate,
    residues,
    doc_lengths,
    residual,
    norm_gain,
):
    tok, chans = query_in.shape
    modes = decay_rate.shape[0]
    tiles = chans // 128
    quarter = modes // YN
    vmem = pl.BlockSpec(memory_space=pltpu.VMEM)
    state = (modes, tiles, 128)
    part = (quarter, tiles, 128)
    dma = pltpu.SemaphoreType.DMA
    return pl.pallas_call(
        functools.partial(block_kernel, nctx, ngrp),
        out_shape=(
            jax.ShapeDtypeStruct((tok, chans), BF16),
            jax.ShapeDtypeStruct((tok, chans), BF16),
        ),
        in_specs=[pl.BlockSpec(memory_space=pltpu.SMEM)] + [vmem] * 8,
        out_specs=(vmem, vmem),
        scratch_shapes=[
            pltpu.VMEM((8, chans), F32),
            pltpu.VMEM((8, chans), F32),
            pltpu.VMEM((tiles * tok, 128), F32),
            pltpu.VMEM((tiles * tok, 128), F32),
            pltpu.VMEM((tiles * tok, 128), F32),
            pltpu.VMEM((tok, 128), F32),
            pltpu.VMEM((tok, 128), F32),
            pltpu.VMEM((nctx, 128), F32),
            pltpu.VMEM((3, tiles * modes, 128), F32),
            pltpu.VMEM(state, F32),
            pltpu.VMEM(state, F32),
            pltpu.VMEM(state, F32),
            pltpu.VMEM(state, F32),
            pltpu.VMEM((YN,) + part, F32),
            pltpu.VMEM(part, F32),
            pltpu.VMEM((BACK,) + part, F32),
            pltpu.VMEM((YN,) + part, F32),
            pltpu.VMEM((YN,) + part, F32),
            pltpu.VMEM((8, 128), F32),
            pltpu.VMEM((ngrp, 8, 128), F32),
            dma,
            dma,
            dma((YN,)),
            dma((YN,)),
            dma((BACK,)),
            dma((BACK,)),
            dma((YN,)),
            dma((YN,)),
            dma((ngrp,)),
            dma((ngrp,)),
        ],
        compiler_params=pltpu.CompilerParams(collective_id=0, has_side_effects=True),
        name="hyena_block",
    )(
        doc_lengths,
        query_in,
        key_in,
        value_in,
        short_taps,
        decay_rate,
        residues,
        residual,
        norm_gain.reshape(1, chans),
    )


def solution(mesh):
    return jax.shard_map(
        functools.partial(shards, mesh.shape["ctx"], mesh.shape["grp"]),
        mesh=mesh,
        in_specs=(
            P("ctx", "grp"),
            P("ctx", "grp"),
            P("ctx", "grp"),
            P(None, None, "grp"),
            P(None, "grp"),
            P(None, "grp"),
            P(),
            P("ctx", "grp"),
            P("grp"),
        ),
        out_specs=(P("ctx", "grp"), P("ctx", "grp")),
        check_vma=False,
    )
```

time: 187 us -> 45.6 us (0.24)
  other arithmetic: 49.4 us -> 0 us
  Pallas kernels: 0 us -> 42.3 us
  local copies, waits for them, and re-layouts: 43 us -> 2.42 us
  waiting for transfers between devices: 32.7 us -> 0 us
  starting transfers between devices: 29.6 us -> 0 us
  blocking collectives: 16.8 us -> 0 us
  matrix products: 7.82 us -> 0 us
  loops' own time: 6 us -> 0 us
    pallas_call x0 -> x1, Pallas kernels: none -> 42.3 us  [shards(): pl.pallas_call(functools.partial(block_kernel, nctx, ngrp), out_shape=(ja...]
    all_to_all x2 -> x0, waiting for transfers between devices: 32.7 us -> none  [the longest x1 17.8 us: shards(): lax.all_to_all(conv_few.astype(jnp.bfloat16), 'ctx', split_axis=1, concat...]
    all_to_all x2 -> x0, starting transfers between devices: 25.6 us -> none  [the longest x1 18.3 us: shards(): lax.all_to_all(gate_cols, 'ctx', split_axis=0, concat_axis=1, tiled=True)]
    mul x14 -> x0, other arithmetic: 24.6 us -> none  [the longest x8 24.3 us: channel_conv(): toeplitz = toeplitz * lower[None]]
    slice x33 -> x0, local copies, waits for them, and re-layouts: 20.1 us -> none  [the longest x28 17.5 us: channel_conv(): lax.associative_scan(combine_maps, (carried, block_ends), axis=2)]
    reduce_sum x8 -> x0, other arithmetic: 17.9 us -> none  [intra_group(): jnp.sum(toeplitz[:, None] * same_doc[None] * gate_grp[:, :, None, :], axi...]
    psum x1 -> x0, blocking collectives: 16.8 us -> none  [shards(): square_sum = lax.psum(jnp.sum(hidden * hidden, axis=1), 'grp')]
    pad x8 -> x0, local copies, waits for them, and re-layouts: 10.6 us -> none  [channel_conv(): lax.associative_scan(combine_maps, (carried, block_ends), axis=2)]
  transfers between devices with their start and end apart: 3 -> 0, of which waited for: 2 -> 0; matrix products, arithmetic and copies ran while one was open for 7% -> 0% of each run, Pallas kernels for 0% -> 0%
where the time goes in v1:
time: 45.6 us; the launch traced here: 45.4 us
  Pallas kernels  42.3 us (93%)
  local copies, waits for them, and re-layouts  2.42 us (5%)
  between operations  0.65 us (1%)
    pallas_call x1, Pallas kernels, shards(): pl.pallas_call(functools.partial(block_kernel, nctx, ngrp), out_shape=(ja...  42.3 us
    unnamed x4, local copies, waits for them, and re-layouts  2.42 us

profile of v1, /device:TPU:1, one launch (start us, length us, event | category | flops | bytes accessed | tf_op | source)
XLA Modules:
  0.0 45.4 jit_solution(17339828989856273867)
XLA Ops:
  0.6 42.3 %hyena_block.1 = (bf16[128,1024]{1,0:T(8,128)(2,1)}, bf16[128,1024]{1,0:T(8,128)(2,1)}) custom-call(s32[32]{0:T(128)} %doc_ref.1, bf16[128,1024]{1,0:T(8,128)(2,1)} %q_ref.1, bf16[128,1024]{1,0:T(8,128)(2,1)} %k_ref.1, bf16[128,1024]{1,0:T(8,128)(2,1)} %v_ref.1, f32[3,3,1024]{2,1,0:T(4,128)} %taps_ref.1, f32[16,1024]{1,0:T(8,128)} %rate_ref.1, ...), custom_call_target="tpu_custom_call" | custom-call | tf_op jit(solution)/shard_map/hyena_block/pallas_call | solution.py:350
  43.0 0.0 copy-start
  43.0 1.7 %copy.13 = bf16[128,1024]{1,0:T(8,128)(2,1)} copy(bf16[128,1024]{1,0:T(8,128)(2,1)} %get-tuple-element.4) | data formatting | bytes 524288
  44.7 0.0 copy-done
  44.7 0.7 %copy.14 = bf16[128,1024]{1,0:T(8,128)(2,1)} copy(bf16[128,1024]{1,0:T(8,128)(2,1)S(1)} %copy-done) | data formatting | bytes 524288
Async XLA Ops:
  43.0 1.7 %copy-start = (bf16[128,1024]{1,0:T(8,128)(2,1)S(1)}, bf16[128,1024]{1,0:T(8,128)(2,1)}, u32[]{:S(2)}) copy-start(bf16[128,1024]{1,0:T(8,128)(2,1)} %get-tuple-element.5) | copy-start | bytes 786436

commit v2 on v1

--- a/solution.py
+++ b/solution.py
@@ -27,6 +27,17 @@
 def block_kernel(
     nctx,
     ngrp,
+    doc_hbm,
+    q_hbm,
+    k_hbm,
+    v_hbm,
+    taps_hbm,
+    rate_hbm,
+    res_hbm,
+    resid_hbm,
+    gain_hbm,
+    hid_hbm,
+    norm_hbm,
     doc_ref,
     q_ref,
     k_ref,
@@ -45,6 +56,7 @@
     y_ref,
     keep_ref,
     pre_ref,
+    late_ref,
     carry_ref,
     nat_ref,
     a_ref,
@@ -58,6 +70,8 @@
     r3_ref,
     ss_ref,
     rs_ref,
+    load_sem,
+    store_sem,
     halo_send,
     halo_recv,
     s1,
@@ -71,6 +85,8 @@
 ):
     tok, chans = q_ref.shape
     lanes = 128
+    sub = 8
+    chunks = tok // sub
     tiles = chans // lanes
     modes = rate_ref.shape[0]
     ndoc = doc_ref.shape[0]
@@ -102,45 +118,54 @@
             barrier, inc=1, device_id={"grp": lax.rem(gi + ngrp - k, ngrp)}, device_id_type=MESH
         )
 
+    pairs = (
+        (doc_hbm, doc_ref),
+        (k_hbm, k_ref),
+        (v_hbm, v_ref),
+        (q_hbm, q_ref),
+        (rate_hbm, rate_ref),
+        (taps_hbm, taps_ref),
+        (res_hbm, res_ref),
+        (resid_hbm, resid_ref),
+        (gain_hbm, gain_ref),
+    )
+    loads = [
+        pltpu.make_async_copy(src, dst, load_sem.at[i]) for i, (src, dst) in enumerate(pairs)
+    ]
+    for copy in loads:
+        copy.start()
+
+    loads[0].wait()
+    row = lax.broadcasted_iota(jnp.int32, (tok, lanes), 0)
+    p0 = me * tok
+    start = jnp.int32(0)
+    first = jnp.int32(tok)
+    last = jnp.int32(-1)
+    before = jnp.int32(0)
+    fresh = jnp.zeros((tok, lanes), F32)
+    for d in range(ndoc):
+        rel = start - p0
+        fresh = jnp.where(row == rel, 1.0, fresh)
+        before = jnp.where(rel == -1, 1, before)
+        first = jnp.where(rel >= 0, jnp.minimum(first, rel), first)
+        last = jnp.where((rel >= 0) & (rel < tok), rel, last)
+        start = start + doc_ref[d]
+    keep_one = 1.0 - fresh
+    keep_ref[...] = keep_one
+    keep_prev = jnp.where(row == 0, (1 - before).astype(F32), pltpu.roll(keep_one, 1, 0))
+    keep_two = keep_one * keep_prev
+    pre_ref[...] = jnp.where(row < first, 1.0, 0.0)
+    late_ref[...] = jnp.where(row >= last, 1.0, 0.0)
+
+    for copy in loads[1:4]:
+        copy.wait()
     for i, ref in enumerate((q_ref, k_ref, v_ref)):
         tail_ref[2 * i : 2 * i + 2, :] = ref[tok - 16 :, :].astype(F32)[14:16]
     tail_ref[6:8, :] = jnp.zeros((2, chans), F32)
-
-    rate = rate_ref[...]
-    for slot, value, dest in (
-        (0, jnp.exp(-rate), a_ref),
-        (1, decay_weight(rate, res_ref[...]), w_ref),
-        (2, rate, rate3_ref),
-    ):
-        for j in range(tiles):
-            nat_ref[slot, j * modes : (j + 1) * modes, :] = value[:, j * lanes : (j + 1) * lanes]
-        for n in range(modes):
-            dest[n] = nat_ref[slot, pl.ds(n, tiles, stride=modes), :]
-
-    row = lax.broadcasted_iota(jnp.int32, (tok, lanes), 0)
-    brow = lax.broadcasted_iota(jnp.int32, (nctx, lanes), 0)
-    p0 = me * tok
-    start = jnp.int32(0)
-    first = jnp.int32(tok)
-    before = jnp.int32(0)
-    fresh = jnp.zeros((tok, lanes), F32)
-    opens = jnp.zeros((nctx, lanes), F32)
-    for d in range(ndoc):
-        rel = start - p0
-        fresh = jnp.where(row == rel, 1.0, fresh)
-        opens = jnp.where(brow == start // tok, 1.0, opens)
-        before = jnp.where(rel == -1, 1, before)
-        first = jnp.where(rel >= 0, jnp.minimum(first, rel), first)
-        start = start + doc_ref[d]
-    keep_one = 1.0 - fresh
-    keep_ref[...] = keep_one
-    pre_ref[...] = jnp.where(row < first, 1.0, 0.0)
-    carry_ref[...] = 1.0 - opens
-    keep_prev = jnp.where(row == 0, (1 - before).astype(F32), pltpu.roll(keep_one, 1, 0))
-    keep_two = keep_one * keep_prev
+    for copy in loads[4:]:
+        copy.wait()
 
     pl.semaphore_wait(barrier, 1 + (YN - 1) + BACK + (ngrp - 1))
-
     halo = pltpu.make_async_remote_copy(
         src_ref=tail_ref,
         dst_ref=halo_ref,
@@ -150,40 +175,65 @@
         device_id_type=MESH,
     )
     halo.start()
-    halo.wait()
-
-    def short(ref, i, j):
+
+    def by_mode(slot, value, dest):
+        for j in range(tiles):
+            nat_ref[slot, j * modes : (j + 1) * modes, :] = value[:, j * lanes : (j + 1) * lanes]
+        for n in range(modes):
+            dest[n] = nat_ref[slot, pl.ds(n, tiles, stride=modes), :]
+
+    rate = rate_ref[...]
+    by_mode(0, jnp.exp(-rate), a_ref)
+    by_mode(2, rate, rate3_ref)
+
+    def short(ref, i, j, rows, rim):
         cols = slice(j * lanes, (j + 1) * lanes)
-        x = ref[:, cols].astype(F32)
-        h0 = halo_ref[2 * i : 2 * i + 1, cols]
-        h1 = halo_ref[2 * i + 1 : 2 * i + 2, cols]
-        one = jnp.where(row == 0, h1, pltpu.roll(x, 1, 0)) * keep_one
-        two = jnp.where(row == 0, h0, jnp.where(row == 1, h1, pltpu.roll(x, 2, 0))) * keep_two
+        x = (ref[:, cols] if rows == tok else ref[0:16, cols]).astype(F32)[0:rows]
+        one = pltpu.roll(x, 1, 0)
+        two = pltpu.roll(x, 2, 0)
+        if rim:
+            at = row[0:rows]
+            h0 = halo_ref[2 * i : 2 * i + 1, cols]
+            h1 = halo_ref[2 * i + 1 : 2 * i + 2, cols]
+            one = jnp.where(at == 0, h1, one)
+            two = jnp.where(at == 0, h0, jnp.where(at == 1, h1, two))
         return (
-            taps_ref[i, 0:1, cols] * x + taps_ref[i, 1:2, cols] * one + taps_ref[i, 2:3, cols] * two
+            taps_ref[i, 0:1, cols] * x
+            + taps_ref[i, 1:2, cols] * (one * keep_one[0:rows])
+            + taps_ref[i, 2:3, cols] * (two * keep_two[0:rows])
         )
 
     for j in range(tiles):
-        gate = short(k_ref, 1, j) * short(v_ref, 2, j)
-        g_ref[j * tok : (j + 1) * tok, :] = gate.astype(BF16).astype(F32)
-
-    def scan_step(t, states):
-        g = g_ref[pl.ds(t, tiles, stride=tok), :]
-        keep = keep_ref[pl.ds(t, 1), :]
-        new = []
-        total = None
-        for n in range(modes):
-            s = (a_ref[n] * keep) * states[n] + g
-            term = w_ref[n] * s
-            total = term if total is None else total + term
-            new.append(s)
-        y_ref[pl.ds(t, tiles, stride=tok), :] = total
-        return tuple(new)
+        gate = short(k_ref, 1, j, tok, False) * short(v_ref, 2, j, tok, False)
+        gate = gate.astype(BF16).astype(F32).reshape(chunks, sub, lanes)
+        g_ref[:, j * sub : (j + 1) * sub, :] = gate
+
+    def gate_at(c, r):
+        return g_ref[c, pl.ds(r, tiles, stride=sub), :]
+
+    def late_gate(c, r):
+        return gate_at(c, r) * late_ref[pl.ds(c * sub + r, 1), :]
+
+    def end_chunk(c, states, first_row=0):
+        for r in range(first_row, sub):
+            g = late_gate(c, r)
+            states = tuple(a_ref[n] * states[n] + g for n in range(modes))
+        return states
 
     zero = jnp.zeros((tiles, lanes), F32)
-    states = lax.fori_loop(0, tok, scan_step, (zero,) * modes, unroll=4)
+    states = end_chunk(0, (zero,) * modes, 2)
+    states = lax.fori_loop(1, chunks, end_chunk, states)
     for n in range(modes):
         e_ref[n] = states[n]
+
+    halo.wait()
+    for j in range(tiles):
+        gate = short(k_ref, 1, j, sub, True) * short(v_ref, 2, j, sub, True)
+        g_ref[0, j * sub : (j + 1) * sub, :] = gate.astype(BF16).astype(F32)
+    g0 = late_gate(0, 0)
+    g1 = late_gate(0, 1)
+    for n in range(modes):
+        e_ref[n] = e_ref[n] + jnp.exp(-float(tok - 2) * rate3_ref[n]) * (g1 + a_ref[n] * g0)
 
     sends = []
     for k in range(1, YN):
@@ -201,8 +251,14 @@
     for copy in sends:
         copy.start()
     r1_ref[0] = e_ref[pl.ds(yy * quarter, quarter)]
-    for j in range(tiles):
-        qs_ref[j * tok : (j + 1) * tok, :] = short(q_ref, 0, j)
+    by_mode(1, decay_weight(rate, res_ref[...]), w_ref)
+    brow = lax.broadcasted_iota(jnp.int32, (nctx, lanes), 0)
+    opens = jnp.zeros((nctx, lanes), F32)
+    start = jnp.int32(0)
+    for d in range(ndoc):
+        opens = jnp.where(brow == start // tok, 1.0, opens)
+        start = start + doc_ref[d]
+    carry_ref[...] = 1.0 - opens
     rate_q = rate3_ref[pl.ds(yy * quarter, quarter)]
     decay_blk = jnp.exp(-float(tok) * rate_q)
     decay_plane = jnp.exp(-float(tok * YN) * rate_q)
@@ -216,6 +272,23 @@
         for j in range(1, YN):
             value = value * carry_of(base + j)
         return value
+
+    def scan_chunk(c, states):
+        for r in range(sub):
+            g = gate_at(c, r)
+            keep = keep_ref[pl.ds(c * sub + r, 1), :]
+            new = []
+            total = None
+            for n in range(modes):
+                s = a_ref[n] * (keep * states[n]) + g
+                term = w_ref[n] * s
+                total = term if total is None else total + term
+                new.append(s)
+            y_ref[c, pl.ds(r, tiles, stride=sub), :] = total
+            states = tuple(new)
+        return states
+
+    states = lax.fori_loop(0, chunks // 4, scan_chunk, (zero,) * modes)
 
     for copy in sends:
         copy.wait()
@@ -238,8 +311,12 @@
                 device_id_type=MESH,
             )
         )
-    for copy in sends:
+    for copy in reversed(sends):
         copy.start()
+    lax.fori_loop(chunks // 4, chunks, scan_chunk, states)
+    for j in range(tiles):
+        cols = slice(j * lanes, (j + 1) * lanes)
+        qs_ref[:, cols] = short(q_ref, 0, j, tok, True)
     for copy in sends:
         copy.wait()
     enter = r2_ref[BACK - 1]
@@ -275,28 +352,26 @@
         for n in range(quarter):
             entering.append(w_ref[m * quarter + n] * part[n])
 
-    def fix_step(t, states):
-        new = []
-        total = None
-        for n in range(modes):
-            s = a_ref[n] * states[n]
-            total = s if total is None else total + s
-            new.append(s)
-        at = pl.ds(t, tiles, stride=tok)
-        y_ref[at, :] = y_ref[at, :] + pre_ref[pl.ds(t, 1), :] * total
-        return tuple(new)
-
-    lax.fori_loop(0, tok, fix_step, tuple(entering), unroll=4)
+    def fix_chunk(c, states):
+        for r in range(sub):
+            states = tuple(a_ref[n] * states[n] for n in range(modes))
+            total = states[0]
+            for n in range(1, modes):
+                total = total + states[n]
+            at = pl.ds(r, tiles, stride=sub)
+            y_ref[c, at, :] = y_ref[c, at, :] + pre_ref[pl.ds(c * sub + r, 1), :] * total
+        return states
+
+    lax.fori_loop(0, chunks, fix_chunk, tuple(entering))
 
     squares = jnp.zeros((tok, lanes), F32)
     for j in range(tiles):
-        rows = slice(j * tok, (j + 1) * tok)
         cols = slice(j * lanes, (j + 1) * lanes)
-        conv = y_ref[rows, :].astype(BF16).astype(F32)
-        hidden = resid_ref[:, cols].astype(F32) + qs_ref[rows, :] * conv
+        conv = y_ref[:, j * sub : (j + 1) * sub, :].reshape(tok, lanes)
+        conv = conv.astype(BF16).astype(F32)
+        hidden = resid_ref[:, cols].astype(F32) + qs_ref[:, cols] * conv
         squares = squares + hidden * hidden
-        qs_ref[rows, :] = hidden
-        hid_ref[:, cols] = hidden.astype(BF16)
+        qs_ref[:, cols] = hidden
     by_token = jnp.sum(squares.T, axis=0, keepdims=True)
     ss_ref[...] = jnp.broadcast_to(by_token, (8, lanes))
     sends = []
@@ -313,6 +388,9 @@
         )
     for copy in sends:
         copy.start()
+    hid_ref[...] = qs_ref[...].astype(BF16)
+    hid_out = pltpu.make_async_copy(hid_ref, hid_hbm, store_sem.at[0])
+    hid_out.start()
     for copy in sends:
         copy.wait()
     total = ss_ref[...]
@@ -321,9 +399,12 @@
     inverse = lax.rsqrt(total * (1.0 / D) + 1e-06)
     inverse = jnp.broadcast_to(inverse[0:1, :], (lanes, tok)).T
     for j in range(tiles):
-        rows = slice(j * tok, (j + 1) * tok)
         cols = slice(j * lanes, (j + 1) * lanes)
-        norm_ref[:, cols] = (qs_ref[rows, :] * inverse * gain_ref[:, cols]).astype(BF16)
+        norm_ref[:, cols] = (qs_ref[:, cols] * inverse * gain_ref[:, cols]).astype(BF16)
+    norm_out = pltpu.make_async_copy(norm_ref, norm_hbm, store_sem.at[1])
+    norm_out.start()
+    hid_out.wait()
+    norm_out.wait()
 
 
 def shards(
@@ -343,9 +424,10 @@
     modes = decay_rate.shape[0]
     tiles = chans // 128
     quarter = modes // YN
-    vmem = pl.BlockSpec(memory_space=pltpu.VMEM)
+    anywhere = pl.BlockSpec(memory_space=pl.ANY)
     state = (modes, tiles, 128)
     part = (quarter, tiles, 128)
+    chunked = (tok // 8, tiles * 8, 128)
     dma = pltpu.SemaphoreType.DMA
     return pl.pallas_call(
         functools.partial(block_kernel, nctx, ngrp),
@@ -353,14 +435,26 @@
             jax.ShapeDtypeStruct((tok, chans), BF16),
             jax.ShapeDtypeStruct((tok, chans), BF16),
         ),
-        in_specs=[pl.BlockSpec(memory_space=pltpu.SMEM)] + [vmem] * 8,
-        out_specs=(vmem, vmem),
+        in_specs=[anywhere] * 9,
+        out_specs=(anywhere, anywhere),
         scratch_shapes=[
+            pltpu.SMEM(doc_lengths.shape, jnp.int32),
+            pltpu.VMEM((tok, chans), BF16),
+            pltpu.VMEM((tok, chans), BF16),
+            pltpu.VMEM((tok, chans), BF16),
+            pltpu.VMEM(short_taps.shape, F32),
+            pltpu.VMEM(decay_rate.shape, F32),
+            pltpu.VMEM(residues.shape, F32),
+            pltpu.VMEM((tok, chans), BF16),
+            pltpu.VMEM((1, chans), F32),
+            pltpu.VMEM((tok, chans), BF16),
+            pltpu.VMEM((tok, chans), BF16),
             pltpu.VMEM((8, chans), F32),
             pltpu.VMEM((8, chans), F32),
-            pltpu.VMEM((tiles * tok, 128), F32),
-            pltpu.VMEM((tiles * tok, 128), F32),
-            pltpu.VMEM((tiles * tok, 128), F32),
+            pltpu.VMEM((tok, chans), F32),
+            pltpu.VMEM(chunked, F32),
+            pltpu.VMEM(chunked, F32),
+            pltpu.VMEM((tok, 128), F32),
             pltpu.VMEM((tok, 128), F32),
             pltpu.VMEM((tok, 128), F32),
             pltpu.VMEM((nctx, 128), F32),
@@ -376,6 +470,8 @@
             pltpu.VMEM((YN,) + part, F32),
             pltpu.VMEM((8, 128), F32),
             pltpu.VMEM((ngrp, 8, 128), F32),
+            dma((9,)),
+            dma((2,)),
             dma,
             dma,
             dma((YN,)),

time: 45.6 us -> 40.9 us (0.90)
  Pallas kernels: 42.3 us -> 37.7 us
    pallas_call x1, Pallas kernels: 42.3 us -> 37.7 us  [shards(): pl.pallas_call(functools.partial(block_kernel, nctx, ngrp), out_shape=(ja...]
where the time goes in v2:
time: 40.9 us; the launch traced here: 40.8 us
  Pallas kernels  37.7 us (92%)
  local copies, waits for them, and re-layouts  2.42 us (6%)
  between operations  0.65 us (2%)
    pallas_call x1, Pallas kernels, shards(): pl.pallas_call(functools.partial(block_kernel, nctx, ngrp), out_shape=(ja...  37.7 us
    unnamed x4, local copies, waits for them, and re-layouts  2.42 us

profile of v2, /device:TPU:1, one launch (start us, length us, event | category | flops | bytes accessed | tf_op | source)
XLA Modules:
  0.0 40.8 jit_solution(3000192288394442234)
XLA Ops:
  0.6 37.7 %hyena_block.1 = (bf16[128,1024]{1,0:T(8,128)(2,1)}, bf16[128,1024]{1,0:T(8,128)(2,1)}) custom-call(s32[32]{0:T(128)} %doc_hbm.1, bf16[128,1024]{1,0:T(8,128)(2,1)} %q_hbm.1, bf16[128,1024]{1,0:T(8,128)(2,1)} %k_hbm.1, bf16[128,1024]{1,0:T(8,128)(2,1)} %v_hbm.1, f32[3,3,1024]{2,1,0:T(4,128)} %taps_hbm.1, f32[16,1024]{1,0:T(8,128)} %rate_hbm.1, ...), custom_call_target="tpu_custom_call" | custom-call | tf_op jit(solution)/shard_map/hyena_block/pallas_call | solution.py:432
  38.3 0.0 copy-start
  38.3 1.7 %copy.13 = bf16[128,1024]{1,0:T(8,128)(2,1)} copy(bf16[128,1024]{1,0:T(8,128)(2,1)} %get-tuple-element.4) | data formatting | bytes 524288
  40.0 0.0 copy-done
  40.1 0.7 %copy.14 = bf16[128,1024]{1,0:T(8,128)(2,1)} copy(bf16[128,1024]{1,0:T(8,128)(2,1)S(1)} %copy-done) | data formatting | bytes 524288
Async XLA Ops:
  38.3 1.7 %copy-start = (bf16[128,1024]{1,0:T(8,128)(2,1)S(1)}, bf16[128,1024]{1,0:T(8,128)(2,1)}, u32[]{:S(2)}) copy-start(bf16[128,1024]{1,0:T(8,128)(2,1)} %get-tuple-element.5) | copy-start | bytes 786436

commit v3 on v2

--- a/solution.py
+++ b/solution.py
@@ -82,6 +82,7 @@
     v3,
     s4,
     v4,
+    ready,
 ):
     tok, chans = q_ref.shape
     lanes = 128
@@ -101,18 +102,23 @@
         return z * YN + lax.rem(yy + k, YN)
 
     def plane(k):
-        return lax.rem(z + k + zn, zn) * YN + yy
+        return (z + k) * YN + yy
 
     barrier = pltpu.get_barrier_semaphore()
-    pl.semaphore_signal(
-        barrier, inc=1, device_id={"ctx": lax.rem(me + nctx - 1, nctx)}, device_id_type=MESH
-    )
+    @pl.when(me > 0)
+    def _():
+        pl.semaphore_signal(barrier, inc=1, device_id={"ctx": me - 1}, device_id_type=MESH)
+
     for k in range(1, YN):
         pl.semaphore_signal(
             barrier, inc=1, device_id={"ctx": in_plane(YN - k)}, device_id_type=MESH
         )
     for k in range(1, BACK + 1):
-        pl.semaphore_signal(barrier, inc=1, device_id={"ctx": plane(-k)}, device_id_type=MESH)
+
+        @pl.when(z + k < zn)
+        def _(k=k):
+            pl.semaphore_signal(barrier, inc=1, device_id={"ctx": plane(k)}, device_id_type=MESH)
+
     for k in range(1, ngrp):
         pl.semaphore_signal(
             barrier, inc=1, device_id={"grp": lax.rem(gi + ngrp - k, ngrp)}, device_id_type=MESH
@@ -165,17 +171,6 @@
     for copy in loads[4:]:
         copy.wait()
 
-    pl.semaphore_wait(barrier, 1 + (YN - 1) + BACK + (ngrp - 1))
-    halo = pltpu.make_async_remote_copy(
-        src_ref=tail_ref,
-        dst_ref=halo_ref,
-        send_sem=halo_send,
-        recv_sem=halo_recv,
-        device_id={"ctx": lax.rem(me + 1, nctx)},
-        device_id_type=MESH,
-    )
-    halo.start()
-
     def by_mode(slot, value, dest):
         for j in range(tiles):
             nat_ref[slot, j * modes : (j + 1) * modes, :] = value[:, j * lanes : (j + 1) * lanes]
@@ -214,6 +209,31 @@
     def late_gate(c, r):
         return gate_at(c, r) * late_ref[pl.ds(c * sub + r, 1), :]
 
+    greeted = (YN - 1) + (ngrp - 1) + jnp.minimum(z, BACK) + jnp.minimum(nctx - 1 - me, 1)
+    pl.semaphore_wait(barrier, greeted)
+    halo = pltpu.make_async_remote_copy(
+        src_ref=tail_ref,
+        dst_ref=halo_ref,
+        send_sem=halo_send,
+        recv_sem=halo_recv,
+        device_id={"ctx": me + 1},
+        device_id_type=MESH,
+    )
+
+    @pl.when(me < nctx - 1)
+    def _():
+        halo.start()
+
+    @pl.when(me == 0)
+    def _():
+        halo_ref[...] = jnp.zeros_like(halo_ref)
+
+    for k in range(1, BACK + 1):
+
+        @pl.when(z >= k)
+        def _(k=k):
+            pl.semaphore_signal(ready, inc=1, device_id={"ctx": plane(-k)}, device_id_type=MESH)
+
     def end_chunk(c, states, first_row=0):
         for r in range(first_row, sub):
             g = late_gate(c, r)
@@ -226,7 +246,18 @@
     for n in range(modes):
         e_ref[n] = states[n]
 
-    halo.wait()
+    by_mode(1, decay_weight(rate, res_ref[...]), w_ref)
+    brow = lax.broadcasted_iota(jnp.int32, (nctx, lanes), 0)
+    opens = jnp.zeros((nctx, lanes), F32)
+    start = jnp.int32(0)
+    for d in range(ndoc):
+        opens = jnp.where(brow == start // tok, 1.0, opens)
+        start = start + doc_ref[d]
+    carry_ref[...] = 1.0 - opens
+    @pl.when(me > 0)
+    def _():
+        halo.wait_recv()
+
     for j in range(tiles):
         gate = short(k_ref, 1, j, sub, True) * short(v_ref, 2, j, sub, True)
         g_ref[0, j * sub : (j + 1) * sub, :] = gate.astype(BF16).astype(F32)
@@ -251,14 +282,6 @@
     for copy in sends:
         copy.start()
     r1_ref[0] = e_ref[pl.ds(yy * quarter, quarter)]
-    by_mode(1, decay_weight(rate, res_ref[...]), w_ref)
-    brow = lax.broadcasted_iota(jnp.int32, (nctx, lanes), 0)
-    opens = jnp.zeros((nctx, lanes), F32)
-    start = jnp.int32(0)
-    for d in range(ndoc):
-        opens = jnp.where(brow == start // tok, 1.0, opens)
-        start = start + doc_ref[d]
-    carry_ref[...] = 1.0 - opens
     rate_q = rate3_ref[pl.ds(yy * quarter, quarter)]
     decay_blk = jnp.exp(-float(tok) * rate_q)
     decay_plane = jnp.exp(-float(tok * YN) * rate_q)
@@ -311,14 +334,31 @@
                 device_id_type=MESH,
             )
         )
-    for copy in reversed(sends):
-        copy.start()
+    totals = sends
+    @pl.when(z < zn - 1)
+    def _():
+        pl.semaphore_wait(ready, jnp.minimum(zn - 1 - z, BACK))
+
+    for k in range(BACK, 0, -1):
+
+        @pl.when(z + k < zn)
+        def _(k=k):
+            totals[k - 1].start()
+
+        @pl.when(z < k)
+        def _(k=k):
+            r2_ref[k - 1] = jnp.zeros(t_ref.shape, F32)
+
     lax.fori_loop(chunks // 4, chunks, scan_chunk, states)
     for j in range(tiles):
         cols = slice(j * lanes, (j + 1) * lanes)
         qs_ref[:, cols] = short(q_ref, 0, j, tok, True)
-    for copy in sends:
-        copy.wait()
+    for k in range(1, BACK + 1):
+
+        @pl.when(z >= k)
+        def _(k=k):
+            totals[k - 1].wait_recv()
+
     enter = r2_ref[BACK - 1]
     for k in range(BACK - 1, 0, -1):
         enter = r2_ref[k - 1] + decay_plane * plane_carry(k) * enter
@@ -403,6 +443,17 @@
         norm_ref[:, cols] = (qs_ref[:, cols] * inverse * gain_ref[:, cols]).astype(BF16)
     norm_out = pltpu.make_async_copy(norm_ref, norm_hbm, store_sem.at[1])
     norm_out.start()
+
+    @pl.when(me < nctx - 1)
+    def _():
+        halo.wait_send()
+
+    for k in range(1, BACK + 1):
+
+        @pl.when(z + k < zn)
+        def _(k=k):
+            totals[k - 1].wait_send()
+
     hid_out.wait()
     norm_out.wait()
 
@@ -482,6 +533,7 @@
             dma((YN,)),
             dma((ngrp,)),
             dma((ngrp,)),
+            pltpu.SemaphoreType.REGULAR,
         ],
         compiler_params=pltpu.CompilerParams(collective_id=0, has_side_effects=True),
         name="hyena_block",

time: 40.9 us -> 31.4 us (0.77)
  the two profiles are of different devices: /device:TPU:1 before, /device:TPU:481 now
where the time goes in v3:
time: 31.4 us; the launch traced here: 31.2 us
  Pallas kernels  28.2 us (90%)
  local copies, waits for them, and re-layouts  2.42 us (8%)
  between operations  0.65 us (2%)
    pallas_call x1, Pallas kernels, shards(): pl.pallas_call(functools.partial(block_kernel, nctx, ngrp), out_shape=(ja...  28.2 us
    unnamed x4, local copies, waits for them, and re-layouts  2.42 us

profile of v3, /device:TPU:481, one launch (start us, length us, event | category | flops | bytes accessed | tf_op | source)
XLA Modules:
  0.0 31.2 jit_solution(8972597912328594179)
XLA Ops:
  0.6 28.2 %hyena_block.1 = (bf16[128,1024]{1,0:T(8,128)(2,1)}, bf16[128,1024]{1,0:T(8,128)(2,1)}) custom-call(s32[32]{0:T(128)} %doc_hbm.1, bf16[128,1024]{1,0:T(8,128)(2,1)} %q_hbm.1, bf16[128,1024]{1,0:T(8,128)(2,1)} %k_hbm.1, bf16[128,1024]{1,0:T(8,128)(2,1)} %v_hbm.1, f32[3,3,1024]{2,1,0:T(4,128)} %taps_hbm.1, f32[16,1024]{1,0:T(8,128)} %rate_hbm.1, ...), custom_call_target="tpu_custom_call" | custom-call | tf_op jit(solution)/shard_map/hyena_block/pallas_call | solution.py:483
  28.8 0.0 copy-start
  28.8 1.7 %copy.13 = bf16[128,1024]{1,0:T(8,128)(2,1)} copy(bf16[128,1024]{1,0:T(8,128)(2,1)} %get-tuple-element.4) | data formatting | bytes 524288
  30.5 0.0 copy-done
  30.5 0.7 %copy.14 = bf16[128,1024]{1,0:T(8,128)(2,1)} copy(bf16[128,1024]{1,0:T(8,128)(2,1)S(1)} %copy-done) | data formatting | bytes 524288
Async XLA Ops:
  28.8 1.7 %copy-start = (bf16[128,1024]{1,0:T(8,128)(2,1)S(1)}, bf16[128,1024]{1,0:T(8,128)(2,1)}, u32[]{:S(2)}) copy-start(bf16[128,1024]{1,0:T(8,128)(2,1)} %get-tuple-element.5) | copy-start | bytes 786436

commit v4 on v3

--- a/solution.py
+++ b/solution.py
@@ -35,9 +35,8 @@
     rate_hbm,
     res_hbm,
     resid_hbm,
-    gain_hbm,
     hid_hbm,
-    norm_hbm,
+    inv_hbm,
     doc_ref,
     q_ref,
     k_ref,
@@ -46,9 +45,7 @@
     rate_ref,
     res_ref,
     resid_ref,
-    gain_ref,
-    hid_ref,
-    norm_ref,
+    inv_ref,
     tail_ref,
     halo_ref,
     qs_ref,
@@ -133,7 +130,6 @@
         (taps_hbm, taps_ref),
         (res_hbm, res_ref),
         (resid_hbm, resid_ref),
-        (gain_hbm, gain_ref),
     )
     loads = [
         pltpu.make_async_copy(src, dst, load_sem.at[i]) for i, (src, dst) in enumerate(pairs)
@@ -311,7 +307,7 @@
             states = tuple(new)
         return states
 
-    states = lax.fori_loop(0, chunks // 4, scan_chunk, (zero,) * modes)
+    states = lax.fori_loop(0, chunks // 2, scan_chunk, (zero,) * modes)
 
     for copy in sends:
         copy.wait()
@@ -349,7 +345,6 @@
         def _(k=k):
             r2_ref[k - 1] = jnp.zeros(t_ref.shape, F32)
 
-    lax.fori_loop(chunks // 4, chunks, scan_chunk, states)
     for j in range(tiles):
         cols = slice(j * lanes, (j + 1) * lanes)
         qs_ref[:, cols] = short(q_ref, 0, j, tok, True)
@@ -383,6 +378,7 @@
     for copy in sends:
         copy.start()
     r3_ref[0] = i_ref[yy]
+    lax.fori_loop(chunks // 2, chunks, scan_chunk, states)
     for copy in sends:
         copy.wait()
 
@@ -428,8 +424,7 @@
         )
     for copy in sends:
         copy.start()
-    hid_ref[...] = qs_ref[...].astype(BF16)
-    hid_out = pltpu.make_async_copy(hid_ref, hid_hbm, store_sem.at[0])
+    hid_out = pltpu.make_async_copy(qs_ref, hid_hbm, store_sem.at[0])
     hid_out.start()
     for copy in sends:
         copy.wait()
@@ -437,12 +432,9 @@
     for k in range(1, ngrp):
         total = total + rs_ref[k]
     inverse = lax.rsqrt(total * (1.0 / D) + 1e-06)
-    inverse = jnp.broadcast_to(inverse[0:1, :], (lanes, tok)).T
-    for j in range(tiles):
-        cols = slice(j * lanes, (j + 1) * lanes)
-        norm_ref[:, cols] = (qs_ref[:, cols] * inverse * gain_ref[:, cols]).astype(BF16)
-    norm_out = pltpu.make_async_copy(norm_ref, norm_hbm, store_sem.at[1])
-    norm_out.start()
+    inv_ref[...] = inverse[0:1, :]
+    inv_out = pltpu.make_async_copy(inv_ref, inv_hbm, store_sem.at[1])
+    inv_out.start()
 
     @pl.when(me < nctx - 1)
     def _():
@@ -455,7 +447,7 @@
             totals[k - 1].wait_send()
 
     hid_out.wait()
-    norm_out.wait()
+    inv_out.wait()
 
 
 def shards(
@@ -480,13 +472,13 @@
     part = (quarter, tiles, 128)
     chunked = (tok // 8, tiles * 8, 128)
     dma = pltpu.SemaphoreType.DMA
-    return pl.pallas_call(
+    hidden, inverse = pl.pallas_call(
         functools.partial(block_kernel, nctx, ngrp),
         out_shape=(
-            jax.ShapeDtypeStruct((tok, chans), BF16),
-            jax.ShapeDtypeStruct((tok, chans), BF16),
+            jax.ShapeDtypeStruct((tok, chans), F32),
+            jax.ShapeDtypeStruct((1, tok), F32),
         ),
-        in_specs=[anywhere] * 9,
+        in_specs=[anywhere] * 8,
         out_specs=(anywhere, anywhere),
         scratch_shapes=[
             pltpu.SMEM(doc_lengths.shape, jnp.int32),
@@ -497,9 +489,7 @@
             pltpu.VMEM(decay_rate.shape, F32),
             pltpu.VMEM(residues.shape, F32),
             pltpu.VMEM((tok, chans), BF16),
-            pltpu.VMEM((1, chans), F32),
-            pltpu.VMEM((tok, chans), BF16),
-            pltpu.VMEM((tok, chans), BF16),
+            pltpu.VMEM((1, tok), F32),
             pltpu.VMEM((8, chans), F32),
             pltpu.VMEM((8, chans), F32),
             pltpu.VMEM((tok, chans), F32),
@@ -521,7 +511,7 @@
             pltpu.VMEM((YN,) + part, F32),
             pltpu.VMEM((8, 128), F32),
             pltpu.VMEM((ngrp, 8, 128), F32),
-            dma((9,)),
+            dma((8,)),
             dma((2,)),
             dma,
             dma,
@@ -546,8 +536,9 @@
         decay_rate,
         residues,
         residual,
-        norm_gain.reshape(1, chans),
     )
+    normed = (hidden * inverse.reshape(tok)[:, None] * norm_gain[None, :]).astype(BF16)
+    return (hidden.astype(BF16), normed)
 
 
 def solution(mesh):

time: 31.4 us -> 31.4 us (level)
  other arithmetic: 0 us -> 2.03 us
  local copies, waits for them, and re-layouts: 2.42 us -> 0.68 us
  Pallas kernels: 28.2 us -> 27.8 us
    convert_element_type x0 -> x1, other arithmetic: none -> 2.03 us  [shards(): (hidden * inverse.reshape(tok)[:, None] * norm_gain[None, :]).astype(BF16)]
    unnamed x4, local copies, waits for them, and re-layouts: 2.42 us -> 0.68 us
    pallas_call x1, Pallas kernels: 28.2 us -> 27.8 us  [shards(): pl.pallas_call(functools.partial(block_kernel, nctx, ngrp), out_shape=(ja...]
where the time goes in v4:
time: 31.4 us; the launch traced here: 31.2 us
  Pallas kernels  27.8 us (89%)
  other arithmetic  2.03 us (6%)
  local copies, waits for them, and re-layouts  0.68 us (2%)
  between operations  0.66 us (2%)
    pallas_call x1, Pallas kernels, shards(): pl.pallas_call(functools.partial(block_kernel, nctx, ngrp), out_shape=(ja...  27.8 us
    convert_element_type x1, other arithmetic, shards(): (hidden * inverse.reshape(tok)[:, None] * norm_gain[None, :]).astype(BF16)  2.03 us
    unnamed x4, local copies, waits for them, and re-layouts  0.68 us

profile of v4, /device:TPU:481, one launch (start us, length us, event | category | flops | bytes accessed | tf_op | source)
XLA Modules:
  0.0 31.2 jit_solution(2222918747776950940)
XLA Ops:
  0.6 27.8 %hyena_block.1 = (f32[128,1024]{1,0:T(8,128)}, f32[1,128]{1,0:T(1,128)}) custom-call(s32[32]{0:T(128)} %doc_hbm.1, bf16[128,1024]{1,0:T(8,128)(2,1)} %q_hbm.1, bf16[128,1024]{1,0:T(8,128)(2,1)} %k_hbm.1, bf16[128,1024]{1,0:T(8,128)(2,1)} %v_hbm.1, f32[3,3,1024]{2,1,0:T(4,128)} %taps_hbm.1, f32[16,1024]{1,0:T(8,128)} %rate_hbm.1, f32[16,1024]{1,0:T(8,128)} %res_hbm.1, ...), custom_call_target="tpu_custom_call" | custom-call | tf_op jit(solution)/shard_map/hyena_block/pallas_call | solution.py:475
  28.5 0.0 copy-start
  28.5 0.0 copy-start.1
  28.5 0.7 %copy-done = f32[1024]{0:T(1024)S(1)} copy-done((f32[1024]{0:T(1024)S(1)}, f32[1024]{0:T(1024)}, u32[]{:S(2)}) %copy-start) | copy-done | bytes 4120
  29.2 0.0 copy-done.1
  29.2 2.0 %multiply_convert_fusion = (bf16[128,1024]{1,0:T(8,128)(2,1)}, bf16[128,1024]{1,0:T(8,128)(2,1)}) fusion(f32[128,1024]{1,0:T(8,128)} %get-tuple-element.4, f32[1024]{0:T(1024)S(1)} %copy-done, f32[128]{0:T(128)S(1)} %bitcast.1), kind=kLoop, calls=%fused_computation | loop fusion | flops 524288 | bytes 1053184 | tf_op jit(solution)/shard_map/convert_element_type | solution.py:540
Async XLA Ops:
  28.5 0.7 %copy-start = (f32[1024]{0:T(1024)S(1)}, f32[1024]{0:T(1024)}, u32[]{:S(2)}) copy-start(f32[1024]{0:T(1024)} %param.17) | copy-start | bytes 12292
  28.5 0.7 %copy-start.1 = (f32[1,128]{1,0:T(1,128)S(1)}, f32[1,128]{1,0:T(1,128)}, u32[]{:S(2)}) copy-start(f32[1,128]{1,0:T(1,128)} %get-tuple-element.5) | copy-start | bytes 1540

commit v5 on v4

--- a/solution.py
+++ b/solution.py
@@ -48,6 +48,8 @@
     inv_ref,
     tail_ref,
     halo_ref,
+    tail16_ref,
+    halo16_ref,
     qs_ref,
     g_ref,
     y_ref,
@@ -62,7 +64,9 @@
     e_ref,
     r1_ref,
     t_ref,
+    t16_ref,
     r2_ref,
+    r216_ref,
     i_ref,
     r3_ref,
     ss_ref,
@@ -164,6 +168,7 @@
     for i, ref in enumerate((q_ref, k_ref, v_ref)):
         tail_ref[2 * i : 2 * i + 2, :] = ref[tok - 16 :, :].astype(F32)[14:16]
     tail_ref[6:8, :] = jnp.zeros((2, chans), F32)
+    tail16_ref[...] = tail_ref[...].astype(BF16)
     for copy in loads[4:]:
         copy.wait()
 
@@ -208,8 +213,8 @@
     greeted = (YN - 1) + (ngrp - 1) + jnp.minimum(z, BACK) + jnp.minimum(nctx - 1 - me, 1)
     pl.semaphore_wait(barrier, greeted)
     halo = pltpu.make_async_remote_copy(
-        src_ref=tail_ref,
-        dst_ref=halo_ref,
+        src_ref=tail16_ref,
+        dst_ref=halo16_ref,
         send_sem=halo_send,
         recv_sem=halo_recv,
         device_id={"ctx": me + 1},
@@ -222,7 +227,7 @@
 
     @pl.when(me == 0)
     def _():
-        halo_ref[...] = jnp.zeros_like(halo_ref)
+        halo16_ref[...] = jnp.zeros(halo16_ref.shape, BF16)
 
     for k in range(1, BACK + 1):
 
@@ -254,6 +259,7 @@
     def _():
         halo.wait_recv()
 
+    halo_ref[...] = halo16_ref[...].astype(F32)
     for j in range(tiles):
         gate = short(k_ref, 1, j, sub, True) * short(v_ref, 2, j, sub, True)
         g_ref[0, j * sub : (j + 1) * sub, :] = gate.astype(BF16).astype(F32)
@@ -317,13 +323,14 @@
     for j in range(1, YN):
         total = ends[j] + decay_blk * carry_of(z * YN + j) * total
     t_ref[...] = total
+    t16_ref[...] = total.astype(BF16)
 
     sends = []
     for k in range(1, BACK + 1):
         sends.append(
             pltpu.make_async_remote_copy(
-                src_ref=t_ref,
-                dst_ref=r2_ref.at[k - 1],
+                src_ref=t_ref if k == 1 else t16_ref,
+                dst_ref=r2_ref if k == 1 else r216_ref.at[k - 2],
                 send_sem=s2.at[k - 1],
                 recv_sem=v2.at[k - 1],
                 device_id={"ctx": plane(k)},
@@ -343,8 +350,12 @@
 
         @pl.when(z < k)
         def _(k=k):
-            r2_ref[k - 1] = jnp.zeros(t_ref.shape, F32)
-
+            if k == 1:
+                r2_ref[...] = jnp.zeros(t_ref.shape, F32)
+            else:
+                r216_ref[k - 2] = jnp.zeros(t_ref.shape, BF16)
+
+    states = lax.fori_loop(chunks // 2, 3 * chunks // 4, scan_chunk, states)
     for j in range(tiles):
         cols = slice(j * lanes, (j + 1) * lanes)
         qs_ref[:, cols] = short(q_ref, 0, j, tok, True)
@@ -354,9 +365,10 @@
         def _(k=k):
             totals[k - 1].wait_recv()
 
-    enter = r2_ref[BACK - 1]
+    enter = r216_ref[BACK - 2].astype(F32)
     for k in range(BACK - 1, 0, -1):
-        enter = r2_ref[k - 1] + decay_plane * plane_carry(k) * enter
+        mine = r2_ref[...] if k == 1 else r216_ref[k - 2].astype(F32)
+        enter = mine + decay_plane * plane_carry(k) * enter
     for j in range(YN):
         i_ref[j] = enter
         if j < YN - 1:
@@ -378,7 +390,7 @@
     for copy in sends:
         copy.start()
     r3_ref[0] = i_ref[yy]
-    lax.fori_loop(chunks // 2, chunks, scan_chunk, states)
+    lax.fori_loop(3 * chunks // 4, chunks, scan_chunk, states)
     for copy in sends:
         copy.wait()
 
@@ -492,6 +504,8 @@
             pltpu.VMEM((1, tok), F32),
             pltpu.VMEM((8, chans), F32),
             pltpu.VMEM((8, chans), F32),
+            pltpu.VMEM((8, chans), BF16),
+            pltpu.VMEM((8, chans), BF16),
             pltpu.VMEM((tok, chans), F32),
             pltpu.VMEM(chunked, F32),
             pltpu.VMEM(chunked, F32),
@@ -506,7 +520,9 @@
             pltpu.VMEM(state, F32),
             pltpu.VMEM((YN,) + part, F32),
             pltpu.VMEM(part, F32),
-            pltpu.VMEM((BACK,) + part, F32),
+            pltpu.VMEM(part, BF16),
+            pltpu.VMEM(part, F32),
+            pltpu.VMEM((BACK - 1,) + part, BF16),
             pltpu.VMEM((YN,) + part, F32),
             pltpu.VMEM((YN,) + part, F32),
             pltpu.VMEM((8, 128), F32),

time: 31.4 us -> 30.8 us (0.981)
  Pallas kernels: 27.8 us -> 27.3 us
    pallas_call x1, Pallas kernels: 27.8 us -> 27.3 us  [shards(): pl.pallas_call(functools.partial(block_kernel, nctx, ngrp), out_shape=(ja...]
where the time goes in v5:
time: 30.8 us; the launch traced here: 30.6 us
  Pallas kernels  27.3 us (89%)
  other arithmetic  2.03 us (7%)
  local copies, waits for them, and re-layouts  0.68 us (2%)
  between operations  0.66 us (2%)
    pallas_call x1, Pallas kernels, shards(): pl.pallas_call(functools.partial(block_kernel, nctx, ngrp), out_shape=(ja...  27.3 us
    convert_element_type x1, other arithmetic, shards(): (hidden * inverse.reshape(tok)[:, None] * norm_gain[None, :]).astype(BF16)  2.03 us
    unnamed x4, local copies, waits for them, and re-layouts  0.68 us

profile of v5, /device:TPU:481, one launch (start us, length us, event | category | flops | bytes accessed | tf_op | source)
XLA Modules:
  0.0 30.6 jit_solution(13732201417975077301)
XLA Ops:
  0.6 27.3 %hyena_block.1 = (f32[128,1024]{1,0:T(8,128)}, f32[1,128]{1,0:T(1,128)}) custom-call(s32[32]{0:T(128)} %doc_hbm.1, bf16[128,1024]{1,0:T(8,128)(2,1)} %q_hbm.1, bf16[128,1024]{1,0:T(8,128)(2,1)} %k_hbm.1, bf16[128,1024]{1,0:T(8,128)(2,1)} %v_hbm.1, f32[3,3,1024]{2,1,0:T(4,128)} %taps_hbm.1, f32[16,1024]{1,0:T(8,128)} %rate_hbm.1, f32[16,1024]{1,0:T(8,128)} %res_hbm.1, ...), custom_call_target="tpu_custom_call" | custom-call | tf_op jit(solution)/shard_map/hyena_block/pallas_call | solution.py:487
  27.9 0.0 copy-start
  27.9 0.0 copy-start.1
  27.9 0.7 %copy-done = f32[1024]{0:T(1024)S(1)} copy-done((f32[1024]{0:T(1024)S(1)}, f32[1024]{0:T(1024)}, u32[]{:S(2)}) %copy-start) | copy-done | bytes 4120
  28.6 0.0 copy-done.1
  28.6 2.0 %multiply_convert_fusion = (bf16[128,1024]{1,0:T(8,128)(2,1)}, bf16[128,1024]{1,0:T(8,128)(2,1)}) fusion(f32[128,1024]{1,0:T(8,128)} %get-tuple-element.4, f32[1024]{0:T(1024)S(1)} %copy-done, f32[128]{0:T(128)S(1)} %bitcast.1), kind=kLoop, calls=%fused_computation | loop fusion | flops 524288 | bytes 1053184 | tf_op jit(solution)/shard_map/convert_element_type | solution.py:556
Async XLA Ops:
  27.9 0.7 %copy-start = (f32[1024]{0:T(1024)S(1)}, f32[1024]{0:T(1024)}, u32[]{:S(2)}) copy-start(f32[1024]{0:T(1024)} %param.17) | copy-start | bytes 12292
  27.9 0.7 %copy-start.1 = (f32[1,128]{1,0:T(1,128)S(1)}, f32[1,128]{1,0:T(1,128)}, u32[]{:S(2)}) copy-start(f32[1,128]{1,0:T(1,128)} %get-tuple-element.5) | copy-start | bytes 1540

commit v6 on v5

--- a/solution.py
+++ b/solution.py
@@ -35,8 +35,8 @@
     rate_hbm,
     res_hbm,
     resid_hbm,
-    hid_hbm,
-    inv_hbm,
+    gain_hbm,
+    out_hbm,
     doc_ref,
     q_ref,
     k_ref,
@@ -45,7 +45,8 @@
     rate_ref,
     res_ref,
     resid_ref,
-    inv_ref,
+    gain_ref,
+    out_ref,
     tail_ref,
     halo_ref,
     tail16_ref,
@@ -134,6 +135,7 @@
         (taps_hbm, taps_ref),
         (res_hbm, res_ref),
         (resid_hbm, resid_ref),
+        (gain_hbm, gain_ref),
     )
     loads = [
         pltpu.make_async_copy(src, dst, load_sem.at[i]) for i, (src, dst) in enumerate(pairs)
@@ -436,7 +438,8 @@
         )
     for copy in sends:
         copy.start()
-    hid_out = pltpu.make_async_copy(qs_ref, hid_hbm, store_sem.at[0])
+    out_ref[0] = qs_ref[...].astype(BF16)
+    hid_out = pltpu.make_async_copy(out_ref.at[0], out_hbm.at[0], store_sem.at[0])
     hid_out.start()
     for copy in sends:
         copy.wait()
@@ -444,9 +447,12 @@
     for k in range(1, ngrp):
         total = total + rs_ref[k]
     inverse = lax.rsqrt(total * (1.0 / D) + 1e-06)
-    inv_ref[...] = inverse[0:1, :]
-    inv_out = pltpu.make_async_copy(inv_ref, inv_hbm, store_sem.at[1])
-    inv_out.start()
+    inverse = jnp.broadcast_to(inverse[0:1, :], (lanes, tok)).T
+    for j in range(tiles):
+        cols = slice(j * lanes, (j + 1) * lanes)
+        out_ref[1, :, cols] = (qs_ref[:, cols] * inverse * gain_ref[:, cols]).astype(BF16)
+    norm_out = pltpu.make_async_copy(out_ref.at[1], out_hbm.at[1], store_sem.at[1])
+    norm_out.start()
 
     @pl.when(me < nctx - 1)
     def _():
@@ -459,7 +465,7 @@
             totals[k - 1].wait_send()
 
     hid_out.wait()
-    inv_out.wait()
+    norm_out.wait()
 
 
 def shards(
@@ -484,14 +490,11 @@
     part = (quarter, tiles, 128)
     chunked = (tok // 8, tiles * 8, 128)
     dma = pltpu.SemaphoreType.DMA
-    hidden, inverse = pl.pallas_call(
+    both = pl.pallas_call(
         functools.partial(block_kernel, nctx, ngrp),
-        out_shape=(
-            jax.ShapeDtypeStruct((tok, chans), F32),
-            jax.ShapeDtypeStruct((1, tok), F32),
-        ),
-        in_specs=[anywhere] * 8,
-        out_specs=(anywhere, anywhere),
+        out_shape=jax.ShapeDtypeStruct((2, tok, chans), BF16),
+        in_specs=[anywhere] * 9,
+        out_specs=anywhere,
         scratch_shapes=[
             pltpu.SMEM(doc_lengths.shape, jnp.int32),
             pltpu.VMEM((tok, chans), BF16),
@@ -501,7 +504,8 @@
             pltpu.VMEM(decay_rate.shape, F32),
             pltpu.VMEM(residues.shape, F32),
             pltpu.VMEM((tok, chans), BF16),
-            pltpu.VMEM((1, tok), F32),
+            pltpu.VMEM((1, chans), F32),
+            pltpu.VMEM((2, tok, chans), BF16),
             pltpu.VMEM((8, chans), F32),
             pltpu.VMEM((8, chans), F32),
             pltpu.VMEM((8, chans), BF16),
@@ -527,7 +531,7 @@
             pltpu.VMEM((YN,) + part, F32),
             pltpu.VMEM((8, 128), F32),
             pltpu.VMEM((ngrp, 8, 128), F32),
-            dma((8,)),
+            dma((9,)),
             dma((2,)),
             dma,
             dma,
@@ -552,9 +556,9 @@
         decay_rate,
         residues,
         residual,
+        norm_gain.reshape(1, chans),
     )
-    normed = (hidden * inverse.reshape(tok)[:, None] * norm_gain[None, :]).astype(BF16)
-    return (hidden.astype(BF16), normed)
+    return (both[0], both[1])
 
 
 def solution(mesh):

time: 30.8 us -> 30.3 us (0.984)
  other arithmetic: 2.03 us -> 0 us
  local copies, waits for them, and re-layouts: 0.68 us -> 1.85 us
    convert_element_type x1 -> x0, other arithmetic: 2.03 us -> none  [shards(): (hidden * inverse.reshape(tok)[:, None] * norm_gain[None, :]).astype(BF16)]
    squeeze x0 -> x1, local copies, waits for them, and re-layouts: none -> 1.85 us  [shards(): return (both[0], both[1])]
    unnamed x4 -> x0, local copies, waits for them, and re-layouts: 0.68 us -> none
    pallas_call x1, Pallas kernels: 27.3 us -> 27.6 us  [shards(): pl.pallas_call(functools.partial(block_kernel, nctx, ngrp), out_shape=jax...]
where the time goes in v6:
time: 30.3 us; the launch traced here: 30.1 us
  Pallas kernels  27.6 us (91%)
  local copies, waits for them, and re-layouts  1.85 us (6%)
  between operations  0.64 us (2%)
    pallas_call x1, Pallas kernels, shards(): pl.pallas_call(functools.partial(block_kernel, nctx, ngrp), out_shape=jax...  27.6 us
    squeeze x1, local copies, waits for them, and re-layouts, shards(): return (both[0], both[1])  1.85 us

profile of v6, /device:TPU:481, one launch (start us, length us, event | category | flops | bytes accessed | tf_op | source)
XLA Modules:
  0.0 30.1 jit_solution(13555731083611341542)
XLA Ops:
  0.6 27.6 %hyena_block.1 = bf16[2,128,1024]{2,1,0:T(8,128)(2,1)} custom-call(s32[32]{0:T(128)} %doc_hbm.1, bf16[128,1024]{1,0:T(8,128)(2,1)} %q_hbm.1, bf16[128,1024]{1,0:T(8,128)(2,1)} %k_hbm.1, bf16[128,1024]{1,0:T(8,128)(2,1)} %v_hbm.1, f32[3,3,1024]{2,1,0:T(4,128)} %taps_hbm.1, f32[16,1024]{1,0:T(8,128)} %rate_hbm.1, f32[16,1024]{1,0:T(8,128)} %res_hbm.1, ...), custom_call_target="tpu_custom_call" | custom-call | tf_op jit(solution)/shard_map/hyena_block/pallas_call | solution.py:493
  28.2 1.9 %slice_bitcast_fusion = (bf16[128,1024]{1,0:T(8,128)(2,1)}, bf16[128,1024]{1,0:T(8,128)(2,1)}) fusion(bf16[2,128,1024]{2,1,0:T(8,128)(2,1)} %hyena_block.1), kind=kLoop, calls=%fused_computation | loop fusion | bytes 1048576 | tf_op jit(solution)/shard_map/squeeze | solution.py:561

commit v7 on v6

--- a/solution.py
+++ b/solution.py
@@ -201,17 +201,6 @@
             + taps_ref[i, 2:3, cols] * (two * keep_two[0:rows])
         )
 
-    for j in range(tiles):
-        gate = short(k_ref, 1, j, tok, False) * short(v_ref, 2, j, tok, False)
-        gate = gate.astype(BF16).astype(F32).reshape(chunks, sub, lanes)
-        g_ref[:, j * sub : (j + 1) * sub, :] = gate
-
-    def gate_at(c, r):
-        return g_ref[c, pl.ds(r, tiles, stride=sub), :]
-
-    def late_gate(c, r):
-        return gate_at(c, r) * late_ref[pl.ds(c * sub + r, 1), :]
-
     greeted = (YN - 1) + (ngrp - 1) + jnp.minimum(z, BACK) + jnp.minimum(nctx - 1 - me, 1)
     pl.semaphore_wait(barrier, greeted)
     halo = pltpu.make_async_remote_copy(
@@ -236,6 +225,17 @@
         @pl.when(z >= k)
         def _(k=k):
             pl.semaphore_signal(ready, inc=1, device_id={"ctx": plane(-k)}, device_id_type=MESH)
+
+    for j in range(tiles):
+        gate = short(k_ref, 1, j, tok, False) * short(v_ref, 2, j, tok, False)
+        gate = gate.astype(BF16).astype(F32).reshape(chunks, sub, lanes)
+        g_ref[:, j * sub : (j + 1) * sub, :] = gate
+
+    def gate_at(c, r):
+        return g_ref[c, pl.ds(r, tiles, stride=sub), :]
+
+    def late_gate(c, r):
+        return gate_at(c, r) * late_ref[pl.ds(c * sub + r, 1), :]
 
     def end_chunk(c, states, first_row=0):
         for r in range(first_row, sub):

time: 30.3 us -> 30.3 us (level)
  no operation moved by 1% of the time
where the time goes in v7:
time: 30.3 us; the launch traced here: 30 us
  Pallas kernels  27.5 us (91%)
  local copies, waits for them, and re-layouts  1.85 us (6%)
  between operations  0.64 us (2%)
    pallas_call x1, Pallas kernels, shards(): pl.pallas_call(functools.partial(block_kernel, nctx, ngrp), out_shape=jax...  27.5 us
    squeeze x1, local copies, waits for them, and re-layouts, shards(): return (both[0], both[1])  1.85 us

profile of v7, /device:TPU:481, one launch (start us, length us, event | category | flops | bytes accessed | tf_op | source)
XLA Modules:
  0.0 30.0 jit_solution(14306051012543207067)
XLA Ops:
  0.6 27.5 %hyena_block.1 = bf16[2,128,1024]{2,1,0:T(8,128)(2,1)} custom-call(s32[32]{0:T(128)} %doc_hbm.1, bf16[128,1024]{1,0:T(8,128)(2,1)} %q_hbm.1, bf16[128,1024]{1,0:T(8,128)(2,1)} %k_hbm.1, bf16[128,1024]{1,0:T(8,128)(2,1)} %v_hbm.1, f32[3,3,1024]{2,1,0:T(4,128)} %taps_hbm.1, f32[16,1024]{1,0:T(8,128)} %rate_hbm.1, f32[16,1024]{1,0:T(8,128)} %res_hbm.1, ...), custom_call_target="tpu_custom_call" | custom-call | tf_op jit(solution)/shard_map/hyena_block/pallas_call | solution.py:493
  28.1 1.9 %slice_bitcast_fusion = (bf16[128,1024]{1,0:T(8,128)(2,1)}, bf16[128,1024]{1,0:T(8,128)(2,1)}) fusion(bf16[2,128,1024]{2,1,0:T(8,128)(2,1)} %hyena_block.1), kind=kLoop, calls=%fused_computation | loop fusion | bytes 1048576 | tf_op jit(solution)/shard_map/squeeze | solution.py:561
